TPU v7x, 32 devices: a whole 2x2x4 slice. The times are simulated.
32 devices in a mesh: dp: 8 (over y, x, core), seq: 4 (over z).
Axes of the slice: x: 2, y: 2, z: 4, core: 2. Of those that a mesh axis runs over, the one named last changes fastest.
Arguments:
- states: bfloat16 [4096, 1280], P(('dp', 'seq')), parts along dimension 0, may hold values from -90 to 90
- token_kind: int32 [4096], P(('dp', 'seq')), parts along dimension 0, may hold values from 0 to 3
- episode: int32 [4096], P(('dp', 'seq')), parts along dimension 0, may hold values from 0 to 3, never falling along the last dimension, each value on 1 to 384 neighbouring positions
- kind_table: bfloat16 [4, 1280], replicated, may hold values from -3 to 3
- w_qkv: bfloat16 [1280, 3072], replicated, may hold values from -0.15625 to 0.15625
- w_out: bfloat16 [1024, 1280], replicated, may hold values from -0.1875 to 0.1875
Outputs:
- attended: bfloat16 [4096, 1280], P(('dp', 'seq')), parts along dimension 0
There are 8 independent parts, one for each index of `dp`. A program takes and returns all parts, laid end to end along the dimension named above; an argument that names none is the same for every part. Nothing has to cross between parts.
All inputs are finite; a program needn't handle non-finite values.
Results may differ from a plain program's by a relative error of at most 0.0055.
The roundings to bfloat16 on the way count: a program that leaves them out, or rounds other values in their place, can miss the bound.
Values may be sent and summed in bfloat16 or wider, within the bound.
No kernel may reach another device: no remote copies, remote signals or barrier semaphores. Data moves between devices by JAX's collectives and lax.ppermute only.
A program may use at most 128 MiB of HBM per device.

v0:
```python
import math

import jax
import jax.numpy as jnp
from jax import lax
from jax.sharding import PartitionSpec as P

HEADS = 16


def absorb(
    running, queries, query_place, query_episode, key_rows, value_rows, key_place, key_episode
):
    maxima, totals, summed = running
    temper = 1.0 / math.sqrt(queries.shape[2])
    scores = (
        jnp.einsum("qhd,khd->hqk", queries, key_rows, preferred_element_type=jnp.float32) * temper
    )
    allowed = (key_place[None, :] <= query_place[:, None]) & (
        key_episode[None, :] == query_episode[:, None]
    )
    scores = jnp.where(allowed[None], scores, -1e30)
    raised = jnp.maximum(maxima, jnp.max(scores, axis=2))
    shrink = jnp.exp(maxima - raised)
    weights = jnp.where(allowed[None], jnp.exp(scores - raised[:, :, None]), 0.0)
    totals = totals * shrink + jnp.sum(weights, axis=2)
    summed = summed * shrink.T[:, :, None] + jnp.einsum(
        "hqk,khd->qhd", weights.astype(jnp.bfloat16), value_rows, preferred_element_type=jnp.float32
    )
    return (raised, totals, summed)


def sweep_keys(
    running, queries, query_place, query_episode, key_rows, value_rows, key_place, key_episode
):
    length = key_rows.shape[0]
    stride = math.gcd(length, 512)

    def visit(number, current):
        offset = number * stride
        keys_here = lax.dynamic_slice_in_dim(key_rows, offset, stride, 0)
        values_here = lax.dynamic_slice_in_dim(value_rows, offset, stride, 0)
        place_here = lax.dynamic_slice_in_dim(key_place, offset, stride, 0)
        episode_here = lax.dynamic_slice_in_dim(key_episode, offset, stride, 0)
        skipped = (place_here[0] > query_place[-1]) | (episode_here[-1] < query_episode[0])
        return lax.cond(
            skipped,
            lambda s: s,
            lambda s: absorb(
                s,
                queries,
                query_place,
                query_episode,
                keys_here,
                values_here,
                place_here,
                episode_here,
            ),
            current,
        )

    return lax.fori_loop(0, length // stride, visit, running)


def fresh_state(count, heads, head_size):
    return (
        jnp.full((heads, count), -1e30, jnp.float32),
        jnp.zeros((heads, count), jnp.float32),
        jnp.zeros((count, heads, head_size), jnp.float32),
    )


def local(states, token_kind, episode, kind_table, w_qkv, w_out):
    rows = states.shape[0]
    kinds = kind_table.shape[0]
    picked = (token_kind[:, None] == jnp.arange(kinds, dtype=jnp.int32)[None, :]).astype(
        jnp.float32
    )
    added = jnp.dot(picked, kind_table.astype(jnp.float32), precision=lax.Precision.HIGHEST)
    inputs = (states.astype(jnp.float32) + added).astype(jnp.bfloat16)
    projected = jnp.dot(inputs, w_qkv, preferred_element_type=jnp.float32).astype(jnp.bfloat16)
    inner = w_out.shape[0]
    head_size = inner // HEADS
    queries = projected[:, :inner].reshape(rows, HEADS, head_size)
    key_flat = projected[:, inner : 2 * inner]
    value_flat = projected[:, 2 * inner :]
    key_three = key_flat.reshape(rows, HEADS, head_size)
    value_three = value_flat.reshape(rows, HEADS, head_size)
    moved_q, moved_k, moved_v = (
        lax.all_to_all(queries, "seq", split_axis=1, concat_axis=0, tiled=True),
        lax.all_to_all(key_three, "seq", split_axis=1, concat_axis=0, tiled=True),
        lax.all_to_all(value_three, "seq", split_axis=1, concat_axis=0, tiled=True),
    )
    whole_episode = lax.all_gather(episode, "seq", axis=0, tiled=True)
    length = moved_q.shape[0]
    local_heads = moved_q.shape[1]
    whole_place = jnp.arange(length, dtype=jnp.int32)
    stride = math.gcd(length, 512)

    def query_block(number, written):
        offset = number * stride
        block_q = lax.dynamic_slice_in_dim(moved_q, offset, stride, 0)
        block_place = lax.dynamic_slice_in_dim(whole_place, offset, stride, 0)
        block_episode = lax.dynamic_slice_in_dim(whole_episode, offset, stride, 0)
        maxima, totals, summed = sweep_keys(
            fresh_state(stride, local_heads, head_size),
            block_q,
            block_place,
            block_episode,
            moved_k,
            moved_v,
            whole_place,
            whole_episode,
        )
        result = (summed / totals.T[:, :, None]).astype(jnp.bfloat16)
        return lax.dynamic_update_slice_in_dim(written, result, offset, 0)

    written = lax.fori_loop(
        0, length // stride, query_block, jnp.zeros((length, local_heads, head_size), jnp.bfloat16)
    )
    heads_out = lax.all_to_all(written, "seq", split_axis=0, concat_axis=1, tiled=True).reshape(
        rows, inner
    )
    return jnp.dot(heads_out, w_out, preferred_element_type=jnp.float32).astype(jnp.bfloat16)


def solution(mesh):
    placed = (P(("dp", "seq"), None), P(("dp", "seq")), P(("dp", "seq")), P(), P(), P())
    return jax.shard_map(
        local, mesh=mesh, in_specs=placed, out_specs=P(("dp", "seq"), None), check_vma=False
    )
```

profile of v0, /device:TPU:0, one launch (start us, length us, event | category | flops | bytes accessed | tf_op | source)
XLA Modules:
  0.0 70.3 jit_solution(8716372642339516466)
XLA Ops:
  0.0 0.0 copy-start
  0.0 1.4 %fusion.23 = bf16[128,1280]{1,0:T(8,128)(2,1)S(1)} fusion(bf16[4,1280]{1,0:T(4,128)(2,1)} %param.11, bf16[128,1280]{1,0:T(8,128)(2,1)} %param.8, s32[128]{0:T(128)} %param.9), kind=kOutput, calls=%fused_computation.26 | convolution fusion | flops 1802752 | bytes 666112 | tf_op jit(solution)/shard_map/dot_general | solution.py:79
  1.4 4.5 %convolution_convert_fusion = bf16[128,3072]{1,0:T(8,128)(2,1)S(1)} fusion(bf16[128,1280]{1,0:T(8,128)(2,1)S(1)} %fusion.23, bf16[1280,3072]{1,0:T(8,128)(2,1)} %param.12), kind=kOutput, calls=%fused_computation.24 | convolution fusion | flops 1007026176 | bytes 8978432 | tf_op jit(solution)/shard_map/dot_general | solution.py:81
  6.0 0.0 copy-start.2
  6.0 0.1 fusion.25
  6.1 0.8 %copy.37 = bf16[128,1024]{0,1:T(8,128)(2,1)} copy(bf16[128,1024]{1,0:T(8,128)(2,1)S(1)} %get-tuple-element.182) | data formatting | bytes 524288 | tf_op jit(solution)/shard_map/slice | solution.py:86
  6.9 6.3 %all-to-all-start.2 = ((bf16[128,16,64]{0,2,1:T(8,128)(2,1)}), bf16[128,16,64]{0,2,1:T(8,128)(2,1)S(1)}, u32[]{:S(2)}, u32[]{:S(2)}) async-start(bf16[128,16,64]{0,2,1:T(8,128)(2,1)} %bitcast.11), calls=%async_computation.2 | async-start | bytes 524288 | tf_op jit(solution)/shard_map/all_to_all | solution.py:92
  13.2 0.8 %copy.36 = bf16[128,1024]{0,1:T(8,128)(2,1)} copy(bf16[128,1024]{1,0:T(8,128)(2,1)S(1)} %get-tuple-element.183) | data formatting | bytes 524288 | tf_op jit(solution)/shard_map/slice | solution.py:85
  14.1 8.1 %all-to-all-done.2 = bf16[128,16,64]{0,2,1:T(8,128)(2,1)S(1)} async-done(((bf16[128,16,64]{0,2,1:T(8,128)(2,1)}), bf16[128,16,64]{0,2,1:T(8,128)(2,1)S(1)}, u32[]{:S(2)}, u32[]{:S(2)}) %all-to-all-start.2) | async-done | bytes 262176 | tf_op jit(solution)/shard_map/all_to_all | solution.py:92
  22.2 3.4 %all-to-all-start.1 = ((bf16[128,16,64]{0,2,1:T(8,128)(2,1)}), bf16[128,16,64]{0,2,1:T(8,128)(2,1)S(1)}, u32[]{:S(2)}, u32[]{:S(2)}) async-start(bf16[128,16,64]{0,2,1:T(8,128)(2,1)} %bitcast.8), calls=%async_computation.1 | async-start | bytes 524288 | tf_op jit(solution)/shard_map/all_to_all | solution.py:91
  25.6 0.8 %copy.35 = bf16[128,1024]{0,1:T(8,128)(2,1)} copy(bf16[128,1024]{1,0:T(8,128)(2,1)S(1)} %get-tuple-element.184) | data formatting | bytes 524288 | tf_op jit(solution)/shard_map/slice | solution.py:84
  26.4 6.2 %all-to-all-done.1 = bf16[128,16,64]{0,2,1:T(8,128)(2,1)S(1)} async-done(((bf16[128,16,64]{0,2,1:T(8,128)(2,1)}), bf16[128,16,64]{0,2,1:T(8,128)(2,1)S(1)}, u32[]{:S(2)}, u32[]{:S(2)}) %all-to-all-start.1) | async-done | bytes 262176 | tf_op jit(solution)/shard_map/all_to_all | solution.py:91
  32.6 0.0 copy-start.1
  32.6 4.0 %all-to-all-start = ((bf16[128,16,64]{0,2,1:T(8,128)(2,1)}), bf16[128,16,64]{0,2,1:T(8,128)(2,1)}, u32[]{:S(2)}, u32[]{:S(2)}) async-start(bf16[128,16,64]{0,2,1:T(8,128)(2,1)} %bitcast.5), calls=%async_computation | async-start | bytes 524288 | tf_op jit(solution)/shard_map/all_to_all | solution.py:90
  36.6 0.0 copy-done.2
  36.6 11.3 %all-gather = s32[4,1,128]{2,1,0:T(1,128)S(1)} all-gather(s32[1,1,128]{2,1,0:T(1,128)S(1)} %bitcast.64), channel_id=1, replica_groups=mesh['dp'=8,'seq'=4] {'seq'}, dimensions={0}, use_global_device_ids=true | all-gather | bytes 2560 | tf_op jit(solution)/shard_map/all_gather | solution.py:94
  47.9 0.6 fusion.26
  49.8 0.6 fusion.27
  51.7 0.0 copy-done.1
  51.7 0.1 broadcast.75
  51.8 0.0 all-to-all-done
  51.8 4.7 %conditional.1 = ((f32[4,512]{1,0:T(4,128)S(1)}, f32[512,4,64]{0,2,1:T(8,128)S(1)})) conditional(s32[]{:T(128)} %bitcast.4, (s32[512]{0:T(512)S(1)}, s32[512]{0:T(512)S(1)}, bf16[4,128,4,64]{1,3,2,0:T(8,128)(2,1)}, bf16[4,128,4,64]{1,3,2,0:T(8,128)(2,1)}, f32[4,512]{1,0:T(4,128)S(1)}, /*index=5*/f32[512,4,64]{0,2,1:T(8,128)S(1)}, ...), branch_computations={%region_0.3_spmd, %region_3.4_spmd} | conditional | flops 283121664 | bytes 15568920 | solution.py:46
  51.8 0.3 compare_and_fusion
  52.1 1.9 %fusion = (f32[4,512]{1,0:T(4,128)S(1)}, f32[4,512,512]{1,2,0:T(8,128)S(1)}) fusion(pred[512,512]{0,1:T(8,128)(4,1)S(1)} %compare_and_fusion, bf16[4,128,4,64]{1,3,2,0:T(8,128)(2,1)} %get-tuple-element.174, bf16[4,128,4,64]{1,3,2,0:T(8,128)(2,1)} %get-tuple-element.173), kind=kOutput, calls=%fused_computation.2 | convolution fusion | flops 137361408 | bytes 4988928 | tf_op jit(solution)/shard_map/while/body/eval_jaxpr/while/body/eval_jaxpr/cond/branch_0_fun/qhd,khd->hqk/dot_general | solution.py:17
  54.0 1.0 %fusion.2 = f32[4,512]{1,0:T(4,128)S(1)} fusion(f32[4,512,512]{1,2,0:T(8,128)S(1)} %get-tuple-element.181, f32[4,512]{1,0:T(4,128)S(1)} %broadcast_maximum_fusion, pred[512,512]{0,1:T(8,128)(4,1)S(1)} %compare_and_fusion), kind=kLoop, calls=%fused_computation.4 | loop fusion | flops 5240832 | bytes 4472832 | tf_op jit(solution)/shard_map/while/body/eval_jaxpr/while/body/eval_jaxpr/cond/branch_0_fun/reduce_sum | solution.py:26
  55.1 1.4 %fusion.9 = f32[512,4,64]{0,2,1:T(8,128)S(1)} fusion(f32[4,512,512]{1,2,0:T(8,128)S(1)} %get-tuple-element.181, f32[4,512]{1,0:T(4,128)S(1)} %broadcast_maximum_fusion, pred[512,512]{0,1:T(8,128)(4,1)S(1)} %compare_and_fusion, f32[512,4,64]{0,2,1:T(8,128)S(1)} %get-tuple-element.144, f32[512,4]{0,1:T(4,128)S(1)} %get-tuple-element.178, ...), kind=kOutput, calls=%fused_computation.8 | convolution fusion | flops 139722752 | bytes 5783552 | tf_op jit(solution)/shard_map/while/body/eval_jaxpr/while/body/eval_jaxpr/cond/branch_0_fun/hqk,khd->qhd/dot_general | solution.py:27
  56.5 0.1 divide_convert_fusion
  56.5 0.3 copy.41
  56.9 0.4 reshape.84
  57.3 10.2 %all_to_all.72 = bf16[4,2,16384]{2,1,0:T(2,128)(2,1)} all-to-all(bf16[4,2,16384]{2,1,0:T(2,128)(2,1)S(1)} %reshape.84), channel_id=1, replica_groups=mesh['dp'=8,'seq'=4] {'seq'}, dimensions={0} | all-to-all | bytes 524288 | tf_op jit(solution)/shard_map/all_to_all | solution.py:121
  67.4 1.3 %reshape.85 = bf16[512,4,64]{2,1,0:T(4,128)(2,1)S(1)} reshape(bf16[4,2,16384]{2,1,0:T(2,128)(2,1)} %all_to_all.72) | data formatting | bytes 524288
  68.8 0.3 copy.43
  69.0 0.0 copy-done
  69.1 1.3 %convolution_convert_fusion.1 = bf16[128,1280]{1,0:T(8,128)(2,1)} fusion(bf16[128,1024]{0,1:T(8,128)(2,1)S(1)} %bitcast.58, bf16[1024,1280]{1,0:T(8,128)(2,1)S(1)} %copy-done), kind=kOutput, calls=%fused_computation.27 | convolution fusion | flops 335708160 | bytes 3211264 | tf_op jit(solution)/shard_map/dot_general | solution.py:124
  (5 shorter events, 0.0 us)
Async XLA Ops:
  0.0 69.0 %copy-start = (bf16[1024,1280]{1,0:T(8,128)(2,1)S(1)}, bf16[1024,1280]{1,0:T(8,128)(2,1)}, u32[]{:S(2)}) copy-start(bf16[1024,1280]{1,0:T(8,128)(2,1)} %param.13) | copy-start | bytes 7864324
  6.0 30.6 %copy-start.2 = (s32[128]{0:T(128)S(1)}, s32[128]{0:T(128)}, u32[]{:S(2)}) copy-start(s32[128]{0:T(128)} %param.10) | copy-start | bytes 1540
  6.9 15.3 %all-to-all-start.2 = ((bf16[128,16,64]{0,2,1:T(8,128)(2,1)}), bf16[128,16,64]{0,2,1:T(8,128)(2,1)S(1)}, u32[]{:S(2)}, u32[]{:S(2)}) async-start(bf16[128,16,64]{0,2,1:T(8,128)(2,1)} %bitcast.11), calls=%async_computation.2 | async-start | bytes 524288 | tf_op jit(solution)/shard_map/all_to_all | solution.py:92
  22.2 10.4 %all-to-all-start.1 = ((bf16[128,16,64]{0,2,1:T(8,128)(2,1)}), bf16[128,16,64]{0,2,1:T(8,128)(2,1)S(1)}, u32[]{:S(2)}, u32[]{:S(2)}) async-start(bf16[128,16,64]{0,2,1:T(8,128)(2,1)} %bitcast.8), calls=%async_computation.1 | async-start | bytes 524288 | tf_op jit(solution)/shard_map/all_to_all | solution.py:91
  32.6 19.1 %copy-start.1 = (bf16[128,16,64]{0,2,1:T(8,128)(2,1)}, bf16[128,16,64]{0,2,1:T(8,128)(2,1)S(1)}, u32[]{:S(2)}) copy-start(bf16[128,16,64]{0,2,1:T(8,128)(2,1)S(1)} %all-to-all-done.1) | copy-start | bytes 786436
  32.6 19.2 %all-to-all-start = ((bf16[128,16,64]{0,2,1:T(8,128)(2,1)}), bf16[128,16,64]{0,2,1:T(8,128)(2,1)}, u32[]{:S(2)}, u32[]{:S(2)}) async-start(bf16[128,16,64]{0,2,1:T(8,128)(2,1)} %bitcast.5), calls=%async_computation | async-start | bytes 524288 | tf_op jit(solution)/shard_map/all_to_all | solution.py:90
where the time goes:
time: 70.9 us; the launch traced here: 70.3 us
  blocking collectives  21.5 us (30%)
  waiting for transfers between devices  14.2 us (20%)
  starting transfers between devices  13.8 us (19%)
  matrix products  10.5 us (15%)
  local copies, waits for them, and re-layouts  6.16 us (9%)
  between operations  2.67 us (4%)
  other arithmetic  1.4 us (2%)
    all_gather x1, blocking collectives, local(): whole_episode = lax.all_gather(episode, 'seq', axis=0, tiled=True)  11.3 us
    all_to_all x1, blocking collectives, local(): lax.all_to_all(written, 'seq', split_axis=0, concat_axis=1, tiled=True)  10.2 us
    all_to_all x1, waiting for transfers between devices, local(): lax.all_to_all(value_three, 'seq', split_axis=1, concat_axis=0, tiled=True)  8.07 us
    all_to_all x1, starting transfers between devices, local(): lax.all_to_all(value_three, 'seq', split_axis=1, concat_axis=0, tiled=True)  6.35 us
    all_to_all x1, waiting for transfers between devices, local(): lax.all_to_all(key_three, 'seq', split_axis=1, concat_axis=0, tiled=True)  6.16 us
    dot_general x1, matrix products, local(): jnp.dot(inputs, w_qkv, preferred_element_type=jnp.float32)  4.53 us
    all_to_all x1, starting transfers between devices, local(): lax.all_to_all(queries, 'seq', split_axis=1, concat_axis=0, tiled=True)  4.04 us
    all_to_all x1, starting transfers between devices, local(): lax.all_to_all(key_three, 'seq', split_axis=1, concat_axis=0, tiled=True)  3.4 us
  transfers between devices with their start and end apart: 3, of which 2 were waited for; matrix products, arithmetic and copies ran while one was open for 4% of the time, Pallas kernels for 0%

commit v1 on v0

v1 whole, which is shorter than its diff:
```python
import functools
import math

import jax
import jax.numpy as jnp
from jax import lax
from jax.experimental import pallas as pl
from jax.experimental.pallas import tpu as pltpu
from jax.sharding import PartitionSpec as P

HEADS = 16
PAIR = 2
CHUNKS = 2
MASKED = -1e30
VMEM = pltpu.VMEM
LIMIT = 40 * 1024 * 1024


def call(body, outs, args, flops, scratch=()):
    moved = sum(a.size * a.dtype.itemsize for a in args)
    return pl.pallas_call(
        body,
        out_shape=outs,
        in_specs=[pl.BlockSpec(memory_space=VMEM)] * len(args),
        out_specs=jax.tree.map(lambda _: pl.BlockSpec(memory_space=VMEM), outs),
        scratch_shapes=list(scratch),
        compiler_params=pltpu.CompilerParams(vmem_limit_bytes=LIMIT),
        cost_estimate=pl.CostEstimate(flops=flops, bytes_accessed=moved, transcendentals=0),
    )(*args)


def shape(dims, dtype):
    return jax.ShapeDtypeStruct(dims, dtype)


def embed_body(states, kinds, table, *outs):
    rows = states.shape[0]
    count = table.shape[0]
    numbers = lax.broadcasted_iota(jnp.int32, (count, rows), 0)
    picked = (numbers == kinds[...]).astype(jnp.bfloat16)
    added = lax.dot_general(
        picked, table[...], (((0,), (0,)), ((), ())), preferred_element_type=jnp.float32
    )
    inputs = (states[...].astype(jnp.float32) + added).astype(jnp.bfloat16)
    size = rows // len(outs)
    for number, out in enumerate(outs):
        out[...] = inputs[number * size : (number + 1) * size]


def fold(first, mask, keys, values_t, wide_q, top, total, acc, factor):
    rows = mask.shape[1]
    head = wide_q.shape[0] // HEADS
    wide_mask = jnp.concatenate([mask] * PAIR, axis=1)
    for pair in range(HEADS // PAIR):
        span = slice(pair * PAIR * head, (pair + 1) * PAIR * head)
        scores = jnp.dot(keys[:, span], wide_q[span, :], preferred_element_type=jnp.float32)
        scores = jnp.where(wide_mask, scores, MASKED)
        here = jnp.max(scores, axis=0, keepdims=True)
        line = slice(pair, pair + 1)
        if first:
            raised = here
        else:
            before = top[line, :]
            raised = jnp.maximum(before, here)
            shrink = jnp.exp2((before - raised) * factor)
        weights = jnp.exp2((scores - raised) * factor)
        added = jnp.sum(weights, axis=0, keepdims=True)
        top[line, :] = raised
        total[line, :] = added if first else total[line, :] * shrink + added
        summed = jnp.dot(
            values_t[span, :], weights.astype(jnp.bfloat16), preferred_element_type=jnp.float32
        )
        for one in range(PAIR):
            place = slice(span.start + one * head, span.start + (one + 1) * head)
            lanes = slice(one * rows, (one + 1) * rows)
            part = summed[one * head : (one + 1) * head, lanes]
            acc[place, :] = part if first else acc[place, :] * shrink[:, lanes] + part


def keys_values(x, w_qkv):
    inner = w_qkv.shape[1] // 3
    keys = jnp.dot(x, w_qkv[:, inner : 2 * inner], preferred_element_type=jnp.float32)
    values = jnp.dot(x, w_qkv[:, 2 * inner :], preferred_element_type=jnp.float32)
    return keys.astype(jnp.bfloat16), values.astype(jnp.bfloat16).T


def own_body(factor, chunks, *refs):
    xs, (ep_row, ep_col, w_qkv), (wide_q, top, total, acc) = (
        refs[:chunks],
        refs[chunks : chunks + 3],
        refs[chunks + 3 :],
    )
    x = jnp.concatenate([r[...] for r in xs], axis=0)
    rows = x.shape[0]
    inner = w_qkv.shape[1] // 3
    head = inner // HEADS
    queries = jnp.dot(x, w_qkv[:, :inner], preferred_element_type=jnp.float32)
    queries = queries.astype(jnp.bfloat16).T
    empty = jnp.zeros((head, rows), jnp.bfloat16)
    for number in range(HEADS):
        one = number % PAIR
        place = slice(number * head, (number + 1) * head)
        parts = [queries[place, :] if k == one else empty for k in range(PAIR)]
        wide_q[place, :] = jnp.concatenate(parts, axis=1)
    keys, values_t = keys_values(x, w_qkv)
    place_k = lax.broadcasted_iota(jnp.int32, (rows, rows), 0)
    place_q = lax.broadcasted_iota(jnp.int32, (rows, rows), 1)
    mask = (place_k <= place_q) & (ep_col[...] == ep_row[...])
    fold(True, mask, keys, values_t, wide_q, top, total, acc, factor)


def step_body(factor, chunks, *refs):
    xs = refs[:chunks]
    ep_row, ep_col, w_qkv, wide_q, top_in, total_in, acc_in, top, total, acc = refs[chunks:]
    x = jnp.concatenate([r[...] for r in xs], axis=0) if chunks > 1 else xs[0][...]
    keys, values_t = keys_values(x, w_qkv)
    mask = ep_col[...] == ep_row[...]
    top[...] = top_in[...]
    total[...] = total_in[...]
    acc[...] = acc_in[...]
    fold(False, mask, keys, values_t, wide_q, top, total, acc, factor)


def finish(total, acc, w_out, out):
    rows = acc.shape[1]
    head = acc.shape[0] // HEADS
    parts = []
    for number in range(HEADS):
        pair, one = divmod(number, PAIR)
        scale = 1.0 / total[pair : pair + 1, one * rows : (one + 1) * rows]
        parts.append((acc[number * head : (number + 1) * head, :] * scale).astype(jnp.bfloat16))
    heads_out = jnp.concatenate(parts, axis=0).T
    out[...] = jnp.dot(heads_out, w_out[...], preferred_element_type=jnp.float32).astype(out.dtype)


def last_body(factor, chunks, *refs):
    w_out, out, top, total, acc = refs[chunks + 7 :]
    step_body(factor, chunks, *refs[: chunks + 7], top, total, acc)
    finish(total, acc, w_out, out)


def local(size, states, token_kind, episode, kind_table, w_qkv, w_out):
    rows, width = states.shape
    inner = w_out.shape[0]
    head = inner // HEADS
    factor = math.log2(math.e) / math.sqrt(head)
    piece = rows // CHUNKS
    xs = call(
        embed_body,
        [shape((piece, width), jnp.bfloat16)] * CHUNKS,
        (states, token_kind.reshape(1, rows), kind_table),
        0,
    )
    known = episode[None]
    reach = 1
    while reach < size:
        pairs = [(i, i + reach) for i in range(size - reach)]
        got = lax.ppermute(known + 1, "seq", pairs) - 1
        known = jnp.concatenate([known, got], axis=0)[:size]
        reach *= 2
    ep_row = episode.reshape(1, rows)
    ep_cols = [known[t].reshape(rows, 1) for t in range(size)]
    f32 = jnp.float32
    state = [
        shape((HEADS // PAIR, PAIR * rows), f32),
        shape((HEADS // PAIR, PAIR * rows), f32),
        shape((inner, rows), f32),
    ]
    unit = 2 * rows * width * inner
    wide_q, *now = call(
        functools.partial(own_body, factor, CHUNKS),
        [shape((inner, PAIR * rows), jnp.bfloat16)] + state,
        (*xs, ep_row, ep_cols[0], w_qkv),
        3 * unit,
    )
    moving = list(xs)
    for hop in range(1, size):
        pairs = [(i, i + 1) for i in range(hop - 1, size - 1)]
        moving = [lax.ppermute(m, "seq", pairs) for m in moving]
        args = (*moving, ep_row, ep_cols[hop], w_qkv, wide_q, *now)
        if hop < size - 1:
            now = call(functools.partial(step_body, factor, CHUNKS), state, args, 2 * unit)
    args = (*args, w_out)
    scratch = [VMEM(s.shape, s.dtype) for s in state]
    return call(
        functools.partial(last_body, factor, CHUNKS),
        shape((rows, w_out.shape[1]), jnp.bfloat16),
        args,
        3 * unit,
        scratch,
    )


def solution(mesh):
    placed = (P(("dp", "seq"), None), P(("dp", "seq")), P(("dp", "seq")), P(), P(), P())
    return jax.shard_map(
        functools.partial(local, mesh.shape["seq"]),
        mesh=mesh,
        in_specs=placed,
        out_specs=P(("dp", "seq"), None),
        check_vma=False,
    )
```

time: 70.9 us -> 41.8 us (0.59)
  the two profiles are of different devices: /device:TPU:0 before, /device:TPU:20 now
where the time goes in v1:
time: 41.8 us; the launch traced here: 41.3 us
  starting transfers between devices  16.6 us (40%)
  local copies, waits for them, and re-layouts  10.5 us (25%)
  Pallas kernels  7.32 us (18%)
  waiting for transfers between devices  5.25 us (13%)
  other arithmetic  1.4 us (3%)
    ppermute x6, starting transfers between devices, local(): moving = [lax.ppermute(m, 'seq', pairs) for m in moving]  11.9 us
    unnamed x16, local copies, waits for them, and re-layouts  9.44 us
    pallas_call x5, Pallas kernels, call(): pl.pallas_call(body, out_shape=outs, in_specs=[pl.BlockSpec(memory_space=...  7.32 us
    ppermute x6, waiting for transfers between devices, local(): moving = [lax.ppermute(m, 'seq', pairs) for m in moving]  5.25 us
    ppermute x2, starting transfers between devices, local(): got = lax.ppermute(known + 1, 'seq', pairs) - 1  4.75 us
    add x2, other arithmetic, local(): got = lax.ppermute(known + 1, 'seq', pairs) - 1  1.4 us
    another operation x5, local copies, waits for them, and re-layouts, local(): ep_cols = [known[t].reshape(rows, 1) for t in range(size)]  1.11 us
  transfers between devices with their start and end apart: 8, of which 2 were waited for; matrix products, arithmetic and copies ran while one was open for 4% of the time, Pallas kernels for 11%

profile of v1, /device:TPU:20, one launch (start us, length us, event | category | flops | bytes accessed | tf_op | source)
XLA Modules:
  0.0 41.3 jit_solution(2642007122142245599)
XLA Ops:
  0.0 0.0 copy-start.5
  0.0 0.7 %add_bitcast_fusion = s32[1,128]{1,0:T(1,128)S(1)} fusion(s32[128]{0:T(128)} %param.8), kind=kLoop, calls=%fused_computation.4 | loop fusion | flops 128 | bytes 1024 | tf_op jit(solution)/shard_map/add | solution.py:158
  0.7 3.5 %collective-permute-start.6 = (s32[1,128]{1,0:T(1,128)S(1)}, s32[1,128]{1,0:T(1,128)S(1)}, u32[]{:S(2)}, u32[]{:S(2)}) collective-permute-start(s32[1,128]{1,0:T(1,128)S(1)} %add_bitcast_fusion), channel_id=1, source_target_pairs={{0,1},{1,2},{2,3},{4,5},{5,6},{6,7},{8,9},{9,10},{10,11},{12,13},{... | collective-permute-start | bytes 1544 | tf_op jit(solution)/shard_map/ppermute | solution.py:158
  4.2 0.0 copy-start.3
  4.2 1.0 %copy-done.3 = bf16[128,1280]{1,0:T(8,128)(2,1)S(1)} copy-done((bf16[128,1280]{1,0:T(8,128)(2,1)S(1)}, bf16[128,1280]{1,0:T(8,128)(2,1)}, u32[]{:S(2)}) %copy-start.3) | copy-done | bytes 327704
  5.2 0.0 copy-start.6
  5.2 0.7 %copy-done.6 = bf16[4,1280]{1,0:T(4,128)(2,1)S(1)} copy-done((bf16[4,1280]{1,0:T(4,128)(2,1)S(1)}, bf16[4,1280]{1,0:T(4,128)(2,1)}, u32[]{:S(2)}) %copy-start.6) | copy-done | bytes 10264
  5.9 0.0 copy-start.7
  5.9 0.7 %copy-done.7 = s32[128]{0:T(128)S(1)} copy-done((s32[128]{0:T(128)S(1)}, s32[128]{0:T(128)}, u32[]{:S(2)}) %copy-start.7) | copy-done | bytes 536
  6.5 0.3 shard_map.64
  6.8 1.9 %collective-permute-start = (bf16[64,1280]{1,0:T(8,128)(2,1)S(1)}, bf16[64,1280]{1,0:T(8,128)(2,1)S(1)}, u32[]{:S(2)}, u32[]{:S(2)}) collective-permute-start(bf16[64,1280]{1,0:T(8,128)(2,1)S(1)} %get-tuple-element.17.refs_0_), channel_id=1, source_target_pairs={{0,1},{1,2},{2,3},{4,5},{5,6},{6,7},{8,9},{9,10},{10,11},{12,13},{... | collective-permute-start | bytes 491528 | tf_op jit(solution)/shard_map/ppermute | solution.py:179
  8.8 1.9 %collective-permute-start.3 = (bf16[64,1280]{1,0:T(8,128)(2,1)S(1)}, bf16[64,1280]{1,0:T(8,128)(2,1)S(1)}, u32[]{:S(2)}, u32[]{:S(2)}) collective-permute-start(bf16[64,1280]{1,0:T(8,128)(2,1)S(1)} %get-tuple-element.18.refs_1_), channel_id=1, source_target_pairs={{0,1},{1,2},{2,3},{4,5},{5,6},{6,7},{8,9},{9,10},{10,11},{12,13},{... | collective-permute-start | bytes 491528 | tf_op jit(solution)/shard_map/ppermute | solution.py:179
  10.7 0.8 %copy.7.refs_3_ = s32[128,1]{1,0:T(8,128)S(1)} copy(s32[128,1]{0,1:T(1,128)} %bitcast.11) | data formatting | bytes 1024 | tf_op jit(solution)/shard_map/reshape;squeeze;broadcast_in_dim | solution.py:162
  11.5 0.0 collective-permute-done.6
  11.5 0.7 %add_add_fusion = s32[2,128]{1,0:T(2,128)S(1)} fusion(s32[1,128]{1,0:T(1,128)S(1)} %get-tuple-element.32, s32[1,128]{1,0:T(1,128)} %bitcast.12), kind=kLoop, calls=%fused_computation | loop fusion | flops 512 | bytes 2048 | tf_op jit(solution)/shard_map/add | solution.py:158
  12.1 1.3 %collective-permute-start.7 = (s32[2,128]{1,0:T(2,128)S(1)}, s32[2,128]{1,0:T(2,128)S(1)}, u32[]{:S(2)}, u32[]{:S(2)}) collective-permute-start(s32[2,128]{1,0:T(2,128)S(1)} %add_add_fusion), channel_id=1, source_target_pairs={{0,2},{1,3},{4,6},{5,7},{8,10},{9,11},{12,14},{13,15},{16,18},{17,... | collective-permute-start | bytes 3080 | tf_op jit(solution)/shard_map/ppermute | solution.py:158
  13.4 0.0 copy-start
  13.4 3.2 %copy-done = bf16[1280,3072]{1,0:T(8,128)(2,1)S(1)} copy-done((bf16[1280,3072]{1,0:T(8,128)(2,1)S(1)}, bf16[1280,3072]{1,0:T(8,128)(2,1)}, u32[]{:S(2)}) %copy-start) | copy-done | bytes 7864344
  16.7 0.0 copy-start.4
  16.7 0.7 %copy-done.4 = s32[128]{0:T(128)S(1)} copy-done((s32[128]{0:T(128)S(1)}, s32[128]{0:T(128)}, u32[]{:S(2)}) %copy-start.4) | copy-done | bytes 536
  17.3 1.7 %shard_map.65 = (bf16[1024,256]{1,0:T(8,128)(2,1)S(1)}, f32[8,256]{1,0:T(8,128)S(1)}, f32[8,256]{1,0:T(8,128)S(1)}, f32[1024,128]{1,0:T(8,128)S(1)}) custom-call(bf16[64,1280]{1,0:T(8,128)(2,1)S(1)} %get-tuple-element.17.refs_0_, bf16[64,1280]{1,0:T(8,128)(2,1)S(1)} %get-tuple-element.18.refs_1_, s32[1,128]{1,0:T(1,128)S(1)} %bitcast.13, ...), custom_call_target="tpu_custom_call" | custom-call | flops 1006632960 | bytes 8193024 | tf_op jit(solution)/shard_map/pallas_call | solution.py:21
  19.0 0.1 copy.8.refs_3_
  19.2 0.0 collective-permute-done.refs_0_
  19.2 1.9 %collective-permute-start.1 = (bf16[64,1280]{1,0:T(8,128)(2,1)S(1)}, bf16[64,1280]{1,0:T(8,128)(2,1)S(1)}, u32[]{:S(2)}, u32[]{:S(2)}) collective-permute-start(bf16[64,1280]{1,0:T(8,128)(2,1)S(1)} %collective-permute-done.refs_0_), channel_id=1, source_target_pairs={{1,2},{2,3},{5,6},{6,7},{9,10},{10,11},{13,14},{14,15},{17,18},{18... | collective-permute-start | bytes 491528 | tf_op jit(solution)/shard_map/ppermute | solution.py:179
  21.1 0.0 collective-permute-done.3.refs_1_
  21.1 1.9 %collective-permute-start.4 = (bf16[64,1280]{1,0:T(8,128)(2,1)S(1)}, bf16[64,1280]{1,0:T(8,128)(2,1)S(1)}, u32[]{:S(2)}, u32[]{:S(2)}) collective-permute-start(bf16[64,1280]{1,0:T(8,128)(2,1)S(1)} %collective-permute-done.3.refs_1_), channel_id=1, source_target_pairs={{1,2},{2,3},{5,6},{6,7},{9,10},{10,11},{13,14},{14,15},{17,18},{18... | collective-permute-start | bytes 491528 | tf_op jit(solution)/shard_map/ppermute | solution.py:179
  23.0 0.0 collective-permute-done.7
  23.1 5.1 %collective-permute-done.1.refs_0_ = bf16[64,1280]{1,0:T(8,128)(2,1)S(1)} collective-permute-done((bf16[64,1280]{1,0:T(8,128)(2,1)S(1)}, bf16[64,1280]{1,0:T(8,128)(2,1)S(1)}, u32[]{:S(2)}, u32[]{:S(2)}) %collective-permute-start.1) | collective-permute-done | bytes 163872 | tf_op jit(solution)/shard_map/ppermute | solution.py:179
  28.1 1.9 %collective-permute-start.2 = (bf16[64,1280]{1,0:T(8,128)(2,1)S(1)}, bf16[64,1280]{1,0:T(8,128)(2,1)S(1)}, u32[]{:S(2)}, u32[]{:S(2)}) collective-permute-start(bf16[64,1280]{1,0:T(8,128)(2,1)S(1)} %collective-permute-done.1.refs_0_), channel_id=1, source_target_pairs={{2,3},{6,7},{10,11},{14,15},{18,19},{22,23},{26,27},{30,31}} | collective-permute-start | bytes 491528 | tf_op jit(solution)/shard_map/ppermute | solution.py:179
  30.1 0.2 collective-permute-done.4.refs_1_
  30.2 2.3 %collective-permute-start.5 = (bf16[64,1280]{1,0:T(8,128)(2,1)S(1)}, bf16[64,1280]{1,0:T(8,128)(2,1)S(1)}, u32[]{:S(2)}, u32[]{:S(2)}) collective-permute-start(bf16[64,1280]{1,0:T(8,128)(2,1)S(1)} %collective-permute-done.4.refs_1_), channel_id=1, source_target_pairs={{2,3},{6,7},{10,11},{14,15},{18,19},{22,23},{26,27},{30,31}} | collective-permute-start | bytes 491528 | tf_op jit(solution)/shard_map/ppermute | solution.py:179
  32.5 0.1 copy.9.refs_3_
  32.6 0.1 copy.10.refs_3_
  32.7 0.0 copy-done.5
  32.7 0.0 copy-start.1
  32.7 3.2 %copy-done.1 = bf16[1280,3072]{1,0:T(8,128)(2,1)S(1)} copy-done((bf16[1280,3072]{1,0:T(8,128)(2,1)S(1)}, bf16[1280,3072]{1,0:T(8,128)(2,1)}, u32[]{:S(2)}) %copy-start.1) | copy-done | bytes 7864344
  36.0 0.0 copy-start.2
  36.0 1.4 %shard_map.66 = (f32[8,256]{1,0:T(8,128)S(1)}, f32[8,256]{1,0:T(8,128)S(1)}, f32[1024,128]{1,0:T(8,128)S(1)}) custom-call(bf16[64,1280]{1,0:T(8,128)(2,1)S(1)} %collective-permute-done.refs_0_, bf16[64,1280]{1,0:T(8,128)(2,1)S(1)} %collective-permute-done.3.refs_1_, s32[1,128]{1,0:T(1,128)S(1)} %bitcast.14, s32[128,1]{1,0:T(8,128)S(1)} %copy.8.refs_3_, ...), custom_call_target="tpu_custom_call" | custom-call | flops 671088640 | bytes 9257984 | tf_op jit(solution)/shard_map/pallas_call | solution.py:21
  37.3 1.4 %shard_map.67 = (f32[8,256]{1,0:T(8,128)S(1)}, f32[8,256]{1,0:T(8,128)S(1)}, f32[1024,128]{1,0:T(8,128)S(1)}) custom-call(bf16[64,1280]{1,0:T(8,128)(2,1)S(1)} %collective-permute-done.1.refs_0_, bf16[64,1280]{1,0:T(8,128)(2,1)S(1)} %collective-permute-done.4.refs_1_, s32[1,128]{1,0:T(1,128)S(1)} %bitcast.15, s32[128,1]{1,0:T(8,128)S(1)} %copy.9.refs_3_, ...), custom_call_target="tpu_custom_call" | custom-call | flops 671088640 | bytes 9257984 | tf_op jit(solution)/shard_map/pallas_call | solution.py:21
  38.7 0.0 collective-permute-done.2.refs_0_
  38.7 0.0 collective-permute-done.5.refs_1_
  38.7 0.0 copy-done.2
  38.8 2.6 %shard_map.68 = bf16[128,1280]{1,0:T(8,128)(2,1)} custom-call(bf16[64,1280]{1,0:T(8,128)(2,1)S(1)} %collective-permute-done.2.refs_0_, bf16[64,1280]{1,0:T(8,128)(2,1)S(1)} %collective-permute-done.5.refs_1_, s32[1,128]{1,0:T(1,128)S(1)} %bitcast.16, s32[128,1]{1,0:T(8,128)S(1)} %copy.10.refs_3_, bf16[1280,3072]{1,0:T(8,128)(2,1)S(1)} %copy-done.1, ...), custom_call_target="tpu_custom_call" | custom-call | flops 1006632960 | bytes 11879424 | tf_op jit(solution)/shard_map/pallas_call | solution.py:21
  (3 shorter events, 0.0 us)
Async XLA Ops:
  0.0 32.7 %copy-start.5 = (s32[128]{0:T(128)S(1)}, s32[128]{0:T(128)}, u32[]{:S(2)}) copy-start(s32[128]{0:T(128)} %param.8) | copy-start | bytes 1540
  0.7 10.7 %collective-permute-start.6 = (s32[1,128]{1,0:T(1,128)S(1)}, s32[1,128]{1,0:T(1,128)S(1)}, u32[]{:S(2)}, u32[]{:S(2)}) collective-permute-start(s32[1,128]{1,0:T(1,128)S(1)} %add_bitcast_fusion), channel_id=1, source_target_pairs={{0,1},{1,2},{2,3},{4,5},{5,6},{6,7},{8,9},{9,10},{10,11},{12,13},{... | collective-permute-start | bytes 1544 | tf_op jit(solution)/shard_map/ppermute | solution.py:158
  4.2 1.0 %copy-start.3 = (bf16[128,1280]{1,0:T(8,128)(2,1)S(1)}, bf16[128,1280]{1,0:T(8,128)(2,1)}, u32[]{:S(2)}) copy-start(bf16[128,1280]{1,0:T(8,128)(2,1)} %states.1) | copy-start | bytes 983044
  5.2 0.7 %copy-start.6 = (bf16[4,1280]{1,0:T(4,128)(2,1)S(1)}, bf16[4,1280]{1,0:T(4,128)(2,1)}, u32[]{:S(2)}) copy-start(bf16[4,1280]{1,0:T(4,128)(2,1)} %table.1) | copy-start | bytes 30724
  5.9 0.7 %copy-start.7 = (s32[128]{0:T(128)S(1)}, s32[128]{0:T(128)}, u32[]{:S(2)}) copy-start(s32[128]{0:T(128)} %param.7) | copy-start | bytes 1540
  6.8 12.3 %collective-permute-start = (bf16[64,1280]{1,0:T(8,128)(2,1)S(1)}, bf16[64,1280]{1,0:T(8,128)(2,1)S(1)}, u32[]{:S(2)}, u32[]{:S(2)}) collective-permute-start(bf16[64,1280]{1,0:T(8,128)(2,1)S(1)} %get-tuple-element.17.refs_0_), channel_id=1, source_target_pairs={{0,1},{1,2},{2,3},{4,5},{5,6},{6,7},{8,9},{9,10},{10,11},{12,13},{... | collective-permute-start | bytes 491528 | tf_op jit(solution)/shard_map/ppermute | solution.py:179
  8.8 12.3 %collective-permute-start.3 = (bf16[64,1280]{1,0:T(8,128)(2,1)S(1)}, bf16[64,1280]{1,0:T(8,128)(2,1)S(1)}, u32[]{:S(2)}, u32[]{:S(2)}) collective-permute-start(bf16[64,1280]{1,0:T(8,128)(2,1)S(1)} %get-tuple-element.18.refs_1_), channel_id=1, source_target_pairs={{0,1},{1,2},{2,3},{4,5},{5,6},{6,7},{8,9},{9,10},{10,11},{12,13},{... | collective-permute-start | bytes 491528 | tf_op jit(solution)/shard_map/ppermute | solution.py:179
  12.1 10.9 %collective-permute-start.7 = (s32[2,128]{1,0:T(2,128)S(1)}, s32[2,128]{1,0:T(2,128)S(1)}, u32[]{:S(2)}, u32[]{:S(2)}) collective-permute-start(s32[2,128]{1,0:T(2,128)S(1)} %add_add_fusion), channel_id=1, source_target_pairs={{0,2},{1,3},{4,6},{5,7},{8,10},{9,11},{12,14},{13,15},{16,18},{17,... | collective-permute-start | bytes 3080 | tf_op jit(solution)/shard_map/ppermute | solution.py:158
  13.4 3.2 %copy-start = (bf16[1280,3072]{1,0:T(8,128)(2,1)S(1)}, bf16[1280,3072]{1,0:T(8,128)(2,1)}, u32[]{:S(2)}) copy-start(bf16[1280,3072]{1,0:T(8,128)(2,1)} %refs_4_.7) | copy-start | bytes 23592964
  16.7 0.7 %copy-start.4 = (s32[128]{0:T(128)S(1)}, s32[128]{0:T(128)}, u32[]{:S(2)}) copy-start(s32[128]{0:T(128)} %param.8) | copy-start | bytes 1540
  19.2 9.0 %collective-permute-start.1 = (bf16[64,1280]{1,0:T(8,128)(2,1)S(1)}, bf16[64,1280]{1,0:T(8,128)(2,1)S(1)}, u32[]{:S(2)}, u32[]{:S(2)}) collective-permute-start(bf16[64,1280]{1,0:T(8,128)(2,1)S(1)} %collective-permute-done.refs_0_), channel_id=1, source_target_pairs={{1,2},{2,3},{5,6},{6,7},{9,10},{10,11},{13,14},{14,15},{17,18},{18... | collective-permute-start | bytes 491528 | tf_op jit(solution)/shard_map/ppermute | solution.py:179
  21.1 9.1 %collective-permute-start.4 = (bf16[64,1280]{1,0:T(8,128)(2,1)S(1)}, bf16[64,1280]{1,0:T(8,128)(2,1)S(1)}, u32[]{:S(2)}, u32[]{:S(2)}) collective-permute-start(bf16[64,1280]{1,0:T(8,128)(2,1)S(1)} %collective-permute-done.3.refs_1_), channel_id=1, source_target_pairs={{1,2},{2,3},{5,6},{6,7},{9,10},{10,11},{13,14},{14,15},{17,18},{18... | collective-permute-start | bytes 491528 | tf_op jit(solution)/shard_map/ppermute | solution.py:179
  28.1 10.6 %collective-permute-start.2 = (bf16[64,1280]{1,0:T(8,128)(2,1)S(1)}, bf16[64,1280]{1,0:T(8,128)(2,1)S(1)}, u32[]{:S(2)}, u32[]{:S(2)}) collective-permute-start(bf16[64,1280]{1,0:T(8,128)(2,1)S(1)} %collective-permute-done.1.refs_0_), channel_id=1, source_target_pairs={{2,3},{6,7},{10,11},{14,15},{18,19},{22,23},{26,27},{30,31}} | collective-permute-start | bytes 491528 | tf_op jit(solution)/shard_map/ppermute | solution.py:179
  30.2 8.5 %collective-permute-start.5 = (bf16[64,1280]{1,0:T(8,128)(2,1)S(1)}, bf16[64,1280]{1,0:T(8,128)(2,1)S(1)}, u32[]{:S(2)}, u32[]{:S(2)}) collective-permute-start(bf16[64,1280]{1,0:T(8,128)(2,1)S(1)} %collective-permute-done.4.refs_1_), channel_id=1, source_target_pairs={{2,3},{6,7},{10,11},{14,15},{18,19},{22,23},{26,27},{30,31}} | collective-permute-start | bytes 491528 | tf_op jit(solution)/shard_map/ppermute | solution.py:179
  32.7 3.2 %copy-start.1 = (bf16[1280,3072]{1,0:T(8,128)(2,1)S(1)}, bf16[1280,3072]{1,0:T(8,128)(2,1)}, u32[]{:S(2)}) copy-start(bf16[1280,3072]{1,0:T(8,128)(2,1)} %refs_4_.7) | copy-start | bytes 23592964
  36.0 2.8 %copy-start.2 = (bf16[1024,1280]{1,0:T(8,128)(2,1)S(1)}, bf16[1024,1280]{1,0:T(8,128)(2,1)}, u32[]{:S(2)}) copy-start(bf16[1024,1280]{1,0:T(8,128)(2,1)} %refs_9_.1) | copy-start | bytes 7864324

commit v2 on v1

v2 whole, which is shorter than its diff:
```python
import functools
import math

import jax
import jax.numpy as jnp
from jax import lax
from jax.experimental import pallas as pl
from jax.experimental.pallas import tpu as pltpu
from jax.sharding import PartitionSpec as P

HEADS = 16
PAIR = 2
LINES = HEADS // PAIR
CHUNKS = 2
TILE = 8
MASKED = -1e30
VMEM = pltpu.VMEM
F32 = jnp.float32
BF16 = jnp.bfloat16
LIMIT = 20 * 1024 * 1024


def shape(dims, dtype):
    return jax.ShapeDtypeStruct(dims, dtype)


def call(body, outs, args, cost, scratch=(), aliases=None):
    return pl.pallas_call(
        body,
        out_shape=outs,
        in_specs=[pl.BlockSpec(memory_space=VMEM)] * len(args),
        out_specs=jax.tree.map(lambda _: pl.BlockSpec(memory_space=VMEM), outs),
        scratch_shapes=list(scratch),
        input_output_aliases=aliases or {},
        compiler_params=pltpu.CompilerParams(vmem_limit_bytes=LIMIT),
        cost_estimate=pl.CostEstimate(flops=cost, bytes_accessed=cost // 300, transcendentals=0),
    )(*args)


def pivot_of(size):
    return size // 2 - 1


def roles(size):
    place = lax.axis_index("seq")
    odd = lax.rem(lax.axis_index("dp"), 2) == 1
    return place, odd, odd & (place == pivot_of(size))


def embed_body(states, kinds, episode, table, first, *others):
    rows, width = states.shape
    count = table.shape[0]
    numbers = lax.broadcasted_iota(jnp.int32, (count, rows), 0)
    picked = (numbers == kinds[...]).astype(BF16)
    added = lax.dot_general(
        picked, table[...], (((0,), (0,)), ((), ())), preferred_element_type=F32
    )
    inputs = (states[...].astype(F32) + added).astype(BF16)
    size = rows // (1 + len(others))
    first[:size, :] = inputs[:size]
    first[size:, :] = jnp.zeros((TILE, width), BF16)
    first[size:, :rows] = jnp.broadcast_to(episode[...].astype(F32), (TILE, rows)).astype(BF16)
    for number, out in enumerate(others, 1):
        out[...] = inputs[number * size : (number + 1) * size]


def block_of(refs):
    first = refs[0]
    size = first.shape[0] - TILE
    rows = size * len(refs)
    x = jnp.concatenate([first[:size, :]] + [r[...] for r in refs[1:]], axis=0)
    return x, first[size : size + 1, :rows].astype(F32)


def same_episode(key_episode, query_episode):
    rows = query_episode.shape[1]
    return jnp.broadcast_to(key_episode, (rows, key_episode.shape[1])).T == query_episode


def fold(first, mask, keys, values_t, wide_q, top, total, acc, factor):
    rows = mask.shape[1]
    head = wide_q.shape[0] // HEADS
    wide_mask = jnp.concatenate([mask] * PAIR, axis=1)
    for pair in range(LINES):
        span = slice(pair * PAIR * head, (pair + 1) * PAIR * head)
        scores = jnp.dot(keys[:, span], wide_q[span, :], preferred_element_type=F32)
        scores = jnp.where(wide_mask, scores, MASKED)
        here = jnp.max(scores, axis=0, keepdims=True)
        line = slice(pair, pair + 1)
        if first:
            raised = here
        else:
            before = top[line, :]
            raised = jnp.maximum(before, here)
            shrink = jnp.exp2((before - raised) * factor)
        weights = jnp.exp2((scores - raised) * factor)
        added = jnp.sum(weights, axis=0, keepdims=True)
        top[line, :] = raised
        total[line, :] = added if first else total[line, :] * shrink + added
        summed = jnp.dot(values_t[span, :], weights.astype(BF16), preferred_element_type=F32)
        for one in range(PAIR):
            place = slice(span.start + one * head, span.start + (one + 1) * head)
            lanes = slice(one * rows, (one + 1) * rows)
            part = summed[one * head : (one + 1) * head, lanes]
            acc[place, :] = part if first else acc[place, :] * shrink[:, lanes] + part


def put_keys_values(x, w_qkv, keys, values_t):
    inner = w_qkv.shape[1] // 3
    k = jnp.dot(x, w_qkv[:, inner : 2 * inner], preferred_element_type=F32)
    keys[...] = k.astype(BF16)
    v = jnp.dot(x, w_qkv[:, 2 * inner :], preferred_element_type=F32)
    values_t[...] = v.astype(BF16).T


def put_queries(x, w_qkv, wide_q):
    inner = w_qkv.shape[1] // 3
    head = inner // HEADS
    queries = jnp.dot(x, w_qkv[:, :inner], preferred_element_type=F32).astype(BF16).T
    empty = jnp.zeros((head, x.shape[0]), BF16)
    for number in range(HEADS):
        one = number % PAIR
        place = slice(number * head, (number + 1) * head)
        parts = [queries[place, :] if k == one else empty for k in range(PAIR)]
        wide_q[place, :] = jnp.concatenate(parts, axis=1)


def own_body(factor, *refs):
    xs, w_qkv, (keys, values_t, wide_q, top, total, acc) = refs[:CHUNKS], refs[CHUNKS], refs[-6:]
    x, episode = block_of(xs)
    rows = x.shape[0]
    put_queries(x, w_qkv, wide_q)
    put_keys_values(x, w_qkv, keys, values_t)
    place_k = lax.broadcasted_iota(jnp.int32, (rows, rows), 0)
    place_q = lax.broadcasted_iota(jnp.int32, (rows, rows), 1)
    mask = (place_k <= place_q) & same_episode(episode, episode)
    fold(True, mask, keys, values_t, wide_q, top, total, acc, factor)


def early_body(size, hop, factor, *refs):
    xs, mine = refs[:CHUNKS], refs[CHUNKS]
    w_qkv, wide_q = refs[CHUNKS + 1 : CHUNKS + 3]
    keys, values_t, top, total, acc = refs[-5:]
    place, odd, _ = roles(size)

    @pl.when(odd & (place >= hop) & (place <= pivot_of(size)))
    def _():
        x, episode = block_of(xs)
        put_keys_values(x, w_qkv, keys, values_t)
        mask = same_episode(episode, mine_episode(mine, x.shape[0]))
        fold(False, mask, keys, values_t, wide_q, top, total, acc, factor)


def mine_episode(first, rows):
    size = first.shape[0] - TILE
    return first[size : size + 1, :rows].astype(F32)


def split_three(value):
    high = value.astype(BF16)
    rest = value - high.astype(F32)
    middle = rest.astype(BF16)
    low = (rest - middle.astype(F32)).astype(BF16)
    return [high, middle, low]


def stacked(value):
    rows = value.shape[1] // PAIR
    return jnp.concatenate([value[:, k * rows : (k + 1) * rows] for k in range(PAIR)], axis=0)


def pack(top, total, acc, out):
    inner, rows = acc.shape
    head = inner // HEADS
    scale = 1.0 / total[...]
    for number in range(HEADS):
        pair, one = divmod(number, PAIR)
        place = slice(number * head, (number + 1) * head)
        lanes = slice(one * rows, (one + 1) * rows)
        out[place, :] = (acc[place, :] * scale[pair : pair + 1, lanes]).astype(BF16)
    parts = split_three(stacked(top[...])) + split_three(stacked(total[...]))
    for number, part in enumerate(parts):
        out[inner + number * HEADS : inner + (number + 1) * HEADS, :] = part


def merge(packed, top, total, acc, factor):
    inner, rows = acc.shape
    head = inner // HEADS

    def read(number):
        start = inner + number * 3 * HEADS
        parts = [
            packed[start + k * HEADS : start + (k + 1) * HEADS, :].astype(F32) for k in range(3)
        ]
        whole = (parts[0] + parts[1]) + parts[2]
        return jnp.concatenate([whole[k * LINES : (k + 1) * LINES] for k in range(PAIR)], axis=1)

    other_top, other_total = read(0), read(1)
    before = top[...]
    raised = jnp.maximum(before, other_top)
    shrink = jnp.exp2((before - raised) * factor)
    weight = jnp.exp2((other_top - raised) * factor) * other_total
    top[...] = raised
    total[...] = total[...] * shrink + weight
    for number in range(HEADS):
        pair, one = divmod(number, PAIR)
        place = slice(number * head, (number + 1) * head)
        line, lanes = slice(pair, pair + 1), slice(one * rows, (one + 1) * rows)
        acc[place, :] = (
            acc[place, :] * shrink[line, lanes] + packed[place, :].astype(F32) * weight[line, lanes]
        )


def step_body(size, hop, blocks, factor, *refs):
    refs = list(refs)
    take = lambda count: [refs.pop(0) for _ in range(count)]
    xs, (mine, w_qkv, wide_q) = take(CHUNKS), take(3)
    firsts, kept = take(blocks), take(2 * blocks)
    take(3)
    top, total, acc, keys, values_t, packed = take(6)
    other_q, other_top, other_total, other_acc = take(4)
    place, odd, pivot = roles(size)

    @pl.when(~odd & (place >= hop))
    def _():
        x, episode = block_of(xs)
        put_keys_values(x, w_qkv, keys, values_t)
        mask = same_episode(episode, mine_episode(mine, x.shape[0]))
        fold(False, mask, keys, values_t, wide_q, top, total, acc, factor)

    @pl.when(pivot)
    def _():
        x, episode = block_of(xs)
        put_queries(x, w_qkv, other_q)
        state = (other_q, other_top, other_total, other_acc)
        for number in range(blocks):
            mask = same_episode(mine_episode(firsts[number], x.shape[0]), episode)
            fold(number == 0, mask, *kept[2 * number : 2 * number + 2], *state, factor)
        pack(other_top, other_total, other_acc, packed)
        put_keys_values(x, w_qkv, keys, values_t)


def finish(total, acc, w_out, out):
    inner, rows = acc.shape
    head = inner // HEADS
    parts = []
    for number in range(HEADS):
        pair, one = divmod(number, PAIR)
        scale = 1.0 / total[pair : pair + 1, one * rows : (one + 1) * rows]
        parts.append((acc[number * head : (number + 1) * head, :] * scale).astype(BF16))
    heads_out = jnp.concatenate(parts, axis=0).T
    out[...] = jnp.dot(heads_out, w_out[...], preferred_element_type=F32).astype(out.dtype)


def last_body(size, hops, returns, factor, *refs):
    refs = list(refs)
    take = lambda count: [refs.pop(0) for _ in range(count)]
    xs, (mine, w_qkv, wide_q) = take(CHUNKS), take(3)
    packed = take(returns)
    top_in, total_in, acc_in, w_out, out = take(5)
    top, total, acc, keys, values_t = take(5)
    place, odd, _ = roles(size)
    top[...] = top_in[...]
    total[...] = total_in[...]
    acc[...] = acc_in[...]

    @pl.when(~odd & (place >= hops))
    def _():
        x, episode = block_of(xs)
        put_keys_values(x, w_qkv, keys, values_t)
        mask = same_episode(episode, mine_episode(mine, x.shape[0]))
        fold(False, mask, keys, values_t, wide_q, top, total, acc, factor)

    for number, part in enumerate(packed, 1):

        @pl.when(odd & (place == pivot_of(size) + number))
        def _(part=part):
            merge(part, top, total, acc, factor)

    finish(total, acc, w_out, out)


def local(groups, size, states, token_kind, episode, kind_table, w_qkv, w_out):
    rows, width = states.shape
    inner = w_out.shape[0]
    head = inner // HEADS
    factor = math.log2(math.e) / math.sqrt(head)
    piece = rows // CHUNKS
    pivot = pivot_of(size)
    hops = size - 1
    later = size - 1 - pivot
    even = [g * size for g in range(0, groups, 2)]
    odds = [g * size for g in range(1, groups, 2)]

    def move(value, pairs):
        return lax.ppermute(value, ("dp", "seq"), pairs)

    unit = 2 * rows * width * inner
    chunks = [shape((piece + TILE, width), BF16)] + [shape((piece, width), BF16)] * (CHUNKS - 1)
    mine = call(
        embed_body,
        chunks,
        (states, token_kind.reshape(1, rows), episode.reshape(1, rows), kind_table),
        4 * unit,
    )

    moving = []
    block = mine
    for hop in range(1, size):
        pairs = [(g + i, g + i + 1) for g in even for i in range(hop - 1, size - 1)]
        pairs += [(g + i, g + i - 1) for g in odds for i in range(pivot + 1, size - hop + 1)]
        block = [move(b, pairs) for b in block]
        moving.append(block)
    early = []
    block = mine
    for hop in range(1, pivot + 1):
        pairs = [(g + i, g + i + 1) for g in odds for i in range(hop - 1, pivot)]
        block = [move(b, pairs) for b in block]
        early.append(block)

    state = [
        shape((LINES, PAIR * rows), F32),
        shape((LINES, PAIR * rows), F32),
        shape((inner, rows), F32),
    ]
    wide = shape((inner, PAIR * rows), BF16)
    pair = [shape((rows, inner), BF16), shape((inner, rows), BF16)]
    keys, values_t, wide_q, *now = call(
        functools.partial(own_body, factor), pair + [wide] + state, (*mine, w_qkv), 3 * unit
    )
    firsts, kept = [mine[0]], [keys, values_t]
    for hop, block in enumerate(early, 1):
        args = (*block, mine[0], w_qkv, wide_q, *now)
        keys, values_t, *now = call(
            functools.partial(early_body, size, hop, factor),
            pair + state,
            args,
            2 * unit,
            aliases={len(args) - 3 + k: 2 + k for k in range(3)},
        )
        firsts, kept = firsts + [block[0]], kept + [keys, values_t]
    returned = []
    for hop, block in enumerate(moving[:-1], 1):
        serve = hop <= later
        args = (*block, mine[0], w_qkv, wide_q, *firsts, *kept, *now)
        outs = state + pair + [shape((inner + 6 * HEADS, rows), BF16)]
        *now, keys, values_t, packed = call(
            functools.partial(step_body, size, hop, len(firsts), factor),
            outs,
            args,
            2 * unit,
            [VMEM(s.shape, s.dtype) for s in [wide] + state],
            {len(args) - 3 + k: k for k in range(3)},
        )
        if serve:
            pairs = [(g + pivot, g + pivot + hop) for g in odds]
            returned.append(move(packed, pairs))
        firsts, kept = firsts + [block[0]], kept + [keys, values_t]
    args = (*moving[-1], mine[0], w_qkv, wide_q, *returned, *now, w_out)
    return call(
        functools.partial(last_body, size, hops, len(returned), factor),
        shape((rows, w_out.shape[1]), BF16),
        args,
        3 * unit,
        [VMEM(s.shape, s.dtype) for s in state + pair],
    )


def solution(mesh):
    placed = (P(("dp", "seq"), None), P(("dp", "seq")), P(("dp", "seq")), P(), P(), P())
    return jax.shard_map(
        functools.partial(local, mesh.shape["dp"], mesh.shape["seq"]),
        mesh=mesh,
        in_specs=placed,
        out_specs=P(("dp", "seq"), None),
        check_vma=False,
    )
```

time: 41.8 us -> 41.3 us (0.988)
  the two profiles are of different devices: /device:TPU:20 before, /device:TPU:30 now
where the time goes in v2:
time: 41.3 us; the launch traced here: 40.9 us
  waiting for transfers between devices  14.2 us (34%)
  starting transfers between devices  10.6 us (26%)
  Pallas kernels  8.31 us (20%)
  local copies, waits for them, and re-layouts  7.68 us (19%)
    ppermute x10, waiting for transfers between devices, move(): return lax.ppermute(value, ('dp', 'seq'), pairs)  14.2 us
    ppermute x10, starting transfers between devices, move(): return lax.ppermute(value, ('dp', 'seq'), pairs)  10.6 us
    pallas_call x6, Pallas kernels, call(): pl.pallas_call(body, out_shape=outs, in_specs=[pl.BlockSpec(memory_space=...  8.31 us
    unnamed x14, local copies, waits for them, and re-layouts  7.68 us
  transfers between devices with their start and end apart: 10, of which 2 were waited for; matrix products, arithmetic and copies ran while one was open for 0% of the time, Pallas kernels for 13%

profile of v2, /device:TPU:30, one launch (start us, length us, event | category | flops | bytes accessed | tf_op | source)
XLA Modules:
  0.0 40.9 jit_solution(13019556728952861143)
XLA Ops:
  0.0 0.0 copy-start.3
  0.0 1.0 %copy-done.3 = bf16[128,1280]{1,0:T(8,128)(2,1)S(1)} copy-done((bf16[128,1280]{1,0:T(8,128)(2,1)S(1)}, bf16[128,1280]{1,0:T(8,128)(2,1)}, u32[]{:S(2)}) %copy-start.3) | copy-done | bytes 327704
  1.0 0.0 copy-start.4
  1.0 0.7 %copy-done.4 = bf16[4,1280]{1,0:T(4,128)(2,1)S(1)} copy-done((bf16[4,1280]{1,0:T(4,128)(2,1)S(1)}, bf16[4,1280]{1,0:T(4,128)(2,1)}, u32[]{:S(2)}) %copy-start.4) | copy-done | bytes 10264
  1.7 0.0 copy-start.5
  1.7 0.7 %copy-done.5 = s32[128]{0:T(128)S(1)} copy-done((s32[128]{0:T(128)S(1)}, s32[128]{0:T(128)}, u32[]{:S(2)}) %copy-start.5) | copy-done | bytes 536
  2.3 0.0 copy-start.6
  2.3 0.7 %copy-done.6 = s32[128]{0:T(128)S(1)} copy-done((s32[128]{0:T(128)S(1)}, s32[128]{0:T(128)}, u32[]{:S(2)}) %copy-start.6) | copy-done | bytes 536
  3.0 0.3 shard_map.64
  3.3 1.3 %collective-permute-start = (bf16[72,1280]{1,0:T(8,128)(2,1)S(1)}, bf16[72,1280]{1,0:T(8,128)(2,1)S(1)}, u32[]{:S(2)}, u32[]{:S(2)}) collective-permute-start(bf16[72,1280]{1,0:T(8,128)(2,1)S(1)} %get-tuple-element.28.refs_0_.refs_2_.refs_5_), channel_id=1, source_target_pairs={{0,1},{1,2},{2,3},{8,9},{9,10},{10,11},{16,17},{17,18},{18,19},{24... | collective-permute-start | bytes 552968 | tf_op jit(solution)/shard_map/ppermute | solution.py:296
  4.6 1.3 %collective-permute-start.3 = (bf16[64,1280]{1,0:T(8,128)(2,1)S(1)}, bf16[64,1280]{1,0:T(8,128)(2,1)S(1)}, u32[]{:S(2)}, u32[]{:S(2)}) collective-permute-start(bf16[64,1280]{1,0:T(8,128)(2,1)S(1)} %get-tuple-element.29.refs_1_), channel_id=1, source_target_pairs={{0,1},{1,2},{2,3},{8,9},{9,10},{10,11},{16,17},{17,18},{18,19},{24... | collective-permute-start | bytes 491528 | tf_op jit(solution)/shard_map/ppermute | solution.py:296
  5.9 0.7 %collective-permute-start.6 = (bf16[72,1280]{1,0:T(8,128)(2,1)S(1)}, bf16[72,1280]{1,0:T(8,128)(2,1)S(1)}, u32[]{:S(2)}, u32[]{:S(2)}) collective-permute-start(bf16[72,1280]{1,0:T(8,128)(2,1)S(1)} %get-tuple-element.28.refs_0_.refs_2_.refs_5_), channel_id=1, source_target_pairs={{4,5},{12,13},{20,21},{28,29}} | collective-permute-start | bytes 552968 | tf_op jit(solution)/shard_map/ppermute | solution.py:296
  6.5 0.7 %collective-permute-start.7 = (bf16[64,1280]{1,0:T(8,128)(2,1)S(1)}, bf16[64,1280]{1,0:T(8,128)(2,1)S(1)}, u32[]{:S(2)}, u32[]{:S(2)}) collective-permute-start(bf16[64,1280]{1,0:T(8,128)(2,1)S(1)} %get-tuple-element.29.refs_1_), channel_id=1, source_target_pairs={{4,5},{12,13},{20,21},{28,29}} | collective-permute-start | bytes 491528 | tf_op jit(solution)/shard_map/ppermute | solution.py:296
  7.2 5.2 %collective-permute-done.3.refs_1_ = bf16[64,1280]{1,0:T(8,128)(2,1)S(1)} collective-permute-done((bf16[64,1280]{1,0:T(8,128)(2,1)S(1)}, bf16[64,1280]{1,0:T(8,128)(2,1)S(1)}, u32[]{:S(2)}, u32[]{:S(2)}) %collective-permute-start.3) | collective-permute-done | bytes 163872 | tf_op jit(solution)/shard_map/ppermute | solution.py:296
  12.5 1.3 %collective-permute-start.4 = (bf16[64,1280]{1,0:T(8,128)(2,1)S(1)}, bf16[64,1280]{1,0:T(8,128)(2,1)S(1)}, u32[]{:S(2)}, u32[]{:S(2)}) collective-permute-start(bf16[64,1280]{1,0:T(8,128)(2,1)S(1)} %collective-permute-done.3.refs_1_), channel_id=1, source_target_pairs={{1,2},{2,3},{9,10},{10,11},{17,18},{18,19},{25,26},{26,27},{6,5},{... | collective-permute-start | bytes 491528 | tf_op jit(solution)/shard_map/ppermute | solution.py:296
  13.7 0.0 collective-permute-done.refs_0_.refs_7_
  13.7 1.3 %collective-permute-start.1 = (bf16[72,1280]{1,0:T(8,128)(2,1)S(1)}, bf16[72,1280]{1,0:T(8,128)(2,1)S(1)}, u32[]{:S(2)}, u32[]{:S(2)}) collective-permute-start(bf16[72,1280]{1,0:T(8,128)(2,1)S(1)} %collective-permute-done.refs_0_.refs_7_), channel_id=1, source_target_pairs={{1,2},{2,3},{9,10},{10,11},{17,18},{18,19},{25,26},{26,27},{6,5},{... | collective-permute-start | bytes 552968 | tf_op jit(solution)/shard_map/ppermute | solution.py:296
  15.0 0.0 copy-start
  15.1 3.2 %copy-done = bf16[1280,3072]{1,0:T(8,128)(2,1)S(1)} copy-done((bf16[1280,3072]{1,0:T(8,128)(2,1)S(1)}, bf16[1280,3072]{1,0:T(8,128)(2,1)}, u32[]{:S(2)}) %copy-start) | copy-done | bytes 7864344
  18.3 0.0 copy-start.1
  18.3 1.7 %shard_map.65 = (bf16[128,1024]{1,0:T(8,128)(2,1)S(1)}, bf16[1024,128]{1,0:T(8,128)(2,1)S(1)}, bf16[1024,256]{1,0:T(8,128)(2,1)S(1)}, f32[8,256]{1,0:T(8,128)S(1...) custom-call(bf16[72,1280]{1,0:T(8,128)(2,1)S(1)} %get-tuple-element.28.refs_0_.refs_2_.refs_5_, ...), custom_call_target="tpu_custom_call" | custom-call | flops 1006632960 | bytes 3355443 | tf_op jit(solution)/shard_map/pallas_call | solution.py:28
  20.0 0.0 collective-permute-done.7.refs_1_
  20.0 0.0 collective-permute-done.6.refs_0_.refs_6_
  20.1 1.5 %copy-done.1 = bf16[1280,3072]{1,0:T(8,128)(2,1)S(1)} copy-done((bf16[1280,3072]{1,0:T(8,128)(2,1)S(1)}, bf16[1280,3072]{1,0:T(8,128)(2,1)}, u32[]{:S(2)}) %copy-start.1) | copy-done | bytes 7864344
  21.5 1.4 %shard_map.67 = (f32[8,256]{1,0:T(8,128)S(1)}, f32[8,256]{1,0:T(8,128)S(1)}, f32[1024,128]{1,0:T(8,128)S(1)}, bf16[128,1024]{1,0:T(8,128)(2,1)S(1)}, bf16[1024,1...) custom-call(bf16[72,1280]{1,0:T(8,128)(2,1)S(1)} %collective-permute, ...), custom_call_target="tpu_custom_call", output_to_operand_aliasing={{0}: (11, {}), {1}: (12, {}), {2}: (13, {})} | custom-call | flops 671088640 | bytes 2236962 | tf_op jit(solution)/shard_map/pallas_call | solution.py:28
  22.9 0.0 copy-start.2
  22.9 0.8 %collective-permute-start.8 = (bf16[1120,128]{1,0:T(8,128)(2,1)S(1)}, bf16[1120,128]{1,0:T(8,128)(2,1)S(1)}, u32[]{:S(2)}, u32[]{:S(2)}) collective-permute-start(bf16[1120,128]{1,0:T(8,128)(2,1)S(1)} %get-tuple-element.41), channel_id=1, source_target_pairs={{5,6},{13,14},{21,22},{29,30}} | collective-permute-start | bytes 860168 | tf_op jit(solution)/shard_map/ppermute | solution.py:296
  23.7 0.0 collective-permute-done.4.refs_1_
  23.8 0.0 collective-permute-done.1.refs_0_
  23.8 2.2 %shard_map.68 = (f32[8,256]{1,0:T(8,128)S(1)}, f32[8,256]{1,0:T(8,128)S(1)}, f32[1024,128]{1,0:T(8,128)S(1)}, bf16[128,1024]{1,0:T(8,128)(2,1)}, bf16[1024,128]{...) custom-call(bf16[72,1280]{1,0:T(8,128)(2,1)S(1)} %collective-permute-done, ...), custom_call_target="tpu_custom_call", output_to_operand_aliasing={{0}: (14, {}), {1}: (15, {}), {2}: (16, {})} | custom-call | flops 671088640 | bytes 2236962 | tf_op jit(solution)/shard_map/pallas_call | solution.py:28
  26.0 0.7 %collective-permute-start.9 = (bf16[1120,128]{1,0:T(8,128)(2,1)S(1)}, bf16[1120,128]{1,0:T(8,128)(2,1)S(1)}, u32[]{:S(2)}, u32[]{:S(2)}) collective-permute-start(bf16[1120,128]{1,0:T(8,128)(2,1)S(1)} %get-tuple-element.47), channel_id=1, source_target_pairs={{5,7},{13,15},{21,23},{29,31}} | collective-permute-start | bytes 860168 | tf_op jit(solution)/shard_map/ppermute | solution.py:296
  26.6 1.3 %collective-permute-start.2 = (bf16[72,1280]{1,0:T(8,128)(2,1)S(1)}, bf16[72,1280]{1,0:T(8,128)(2,1)S(1)}, u32[]{:S(2)}, u32[]{:S(2)}) collective-permute-start(bf16[72,1280]{1,0:T(8,128)(2,1)S(1)} %collective-permute-done.1.refs_0_), channel_id=1, source_target_pairs={{2,3},{10,11},{18,19},{26,27}} | collective-permute-start | bytes 552968 | tf_op jit(solution)/shard_map/ppermute | solution.py:296
  27.9 1.3 %collective-permute-start.5 = (bf16[64,1280]{1,0:T(8,128)(2,1)S(1)}, bf16[64,1280]{1,0:T(8,128)(2,1)S(1)}, u32[]{:S(2)}, u32[]{:S(2)}) collective-permute-start(bf16[64,1280]{1,0:T(8,128)(2,1)S(1)} %collective-permute-done.4.refs_1_), channel_id=1, source_target_pairs={{2,3},{10,11},{18,19},{26,27}} | collective-permute-start | bytes 491528 | tf_op jit(solution)/shard_map/ppermute | solution.py:296
  29.2 0.0 collective-permute-done.8.refs_5_
  29.3 8.9 %collective-permute-done.5.refs_1_ = bf16[64,1280]{1,0:T(8,128)(2,1)S(1)} collective-permute-done((bf16[64,1280]{1,0:T(8,128)(2,1)S(1)}, bf16[64,1280]{1,0:T(8,128)(2,1)S(1)}, u32[]{:S(2)}, u32[]{:S(2)}) %collective-permute-start.5) | collective-permute-done | bytes 163872 | tf_op jit(solution)/shard_map/ppermute | solution.py:296
  38.2 0.0 collective-permute-done.2.refs_0_
  38.2 0.0 collective-permute-done.9.refs_6_
  38.2 0.0 copy-done.2
  38.2 2.7 %shard_map.69 = bf16[128,1280]{1,0:T(8,128)(2,1)} custom-call(bf16[72,1280]{1,0:T(8,128)(2,1)S(1)} %collective-permute-done.2.refs_0_, bf16[64,1280]{1,0:T(8,128)(2,1)S(1)} %collective-permute-done.5.refs_1_, bf16[72,1280]{1,0:T(8,128)(2,1)S(1)} %get-tuple-element.28.refs_0_.refs_2_.refs_5_, bf16[1280,3072]{1,0:T(8,128)(2,1)S(1)} %copy-done.1, ...), custom_call_target="tpu_custom_call" | custom-call | flops 1006632960 | bytes 3355443 | tf_op jit(solution)/shard_map/pallas_call | solution.py:28
  (1 shorter events, 0.0 us)
Async XLA Ops:
  0.0 1.0 %copy-start.3 = (bf16[128,1280]{1,0:T(8,128)(2,1)S(1)}, bf16[128,1280]{1,0:T(8,128)(2,1)}, u32[]{:S(2)}) copy-start(bf16[128,1280]{1,0:T(8,128)(2,1)} %states.1) | copy-start | bytes 983044
  1.0 0.7 %copy-start.4 = (bf16[4,1280]{1,0:T(4,128)(2,1)S(1)}, bf16[4,1280]{1,0:T(4,128)(2,1)}, u32[]{:S(2)}) copy-start(bf16[4,1280]{1,0:T(4,128)(2,1)} %table.1) | copy-start | bytes 30724
  1.7 0.7 %copy-start.5 = (s32[128]{0:T(128)S(1)}, s32[128]{0:T(128)}, u32[]{:S(2)}) copy-start(s32[128]{0:T(128)} %param.7) | copy-start | bytes 1540
  2.3 0.7 %copy-start.6 = (s32[128]{0:T(128)S(1)}, s32[128]{0:T(128)}, u32[]{:S(2)}) copy-start(s32[128]{0:T(128)} %param.8) | copy-start | bytes 1540
  3.3 10.5 %collective-permute-start = (bf16[72,1280]{1,0:T(8,128)(2,1)S(1)}, bf16[72,1280]{1,0:T(8,128)(2,1)S(1)}, u32[]{:S(2)}, u32[]{:S(2)}) collective-permute-start(bf16[72,1280]{1,0:T(8,128)(2,1)S(1)} %get-tuple-element.28.refs_0_.refs_2_.refs_5_), channel_id=1, source_target_pairs={{0,1},{1,2},{2,3},{8,9},{9,10},{10,11},{16,17},{17,18},{18,19},{24... | collective-permute-start | bytes 552968 | tf_op jit(solution)/shard_map/ppermute | solution.py:296
  4.6 7.9 %collective-permute-start.3 = (bf16[64,1280]{1,0:T(8,128)(2,1)S(1)}, bf16[64,1280]{1,0:T(8,128)(2,1)S(1)}, u32[]{:S(2)}, u32[]{:S(2)}) collective-permute-start(bf16[64,1280]{1,0:T(8,128)(2,1)S(1)} %get-tuple-element.29.refs_1_), channel_id=1, source_target_pairs={{0,1},{1,2},{2,3},{8,9},{9,10},{10,11},{16,17},{17,18},{18,19},{24... | collective-permute-start | bytes 491528 | tf_op jit(solution)/shard_map/ppermute | solution.py:296
  5.9 14.2 %collective-permute-start.6 = (bf16[72,1280]{1,0:T(8,128)(2,1)S(1)}, bf16[72,1280]{1,0:T(8,128)(2,1)S(1)}, u32[]{:S(2)}, u32[]{:S(2)}) collective-permute-start(bf16[72,1280]{1,0:T(8,128)(2,1)S(1)} %get-tuple-element.28.refs_0_.refs_2_.refs_5_), channel_id=1, source_target_pairs={{4,5},{12,13},{20,21},{28,29}} | collective-permute-start | bytes 552968 | tf_op jit(solution)/shard_map/ppermute | solution.py:296
  6.5 13.5 %collective-permute-start.7 = (bf16[64,1280]{1,0:T(8,128)(2,1)S(1)}, bf16[64,1280]{1,0:T(8,128)(2,1)S(1)}, u32[]{:S(2)}, u32[]{:S(2)}) collective-permute-start(bf16[64,1280]{1,0:T(8,128)(2,1)S(1)} %get-tuple-element.29.refs_1_), channel_id=1, source_target_pairs={{4,5},{12,13},{20,21},{28,29}} | collective-permute-start | bytes 491528 | tf_op jit(solution)/shard_map/ppermute | solution.py:296
  12.5 11.3 %collective-permute-start.4 = (bf16[64,1280]{1,0:T(8,128)(2,1)S(1)}, bf16[64,1280]{1,0:T(8,128)(2,1)S(1)}, u32[]{:S(2)}, u32[]{:S(2)}) collective-permute-start(bf16[64,1280]{1,0:T(8,128)(2,1)S(1)} %collective-permute-done.3.refs_1_), channel_id=1, source_target_pairs={{1,2},{2,3},{9,10},{10,11},{17,18},{18,19},{25,26},{26,27},{6,5},{... | collective-permute-start | bytes 491528 | tf_op jit(solution)/shard_map/ppermute | solution.py:296
  13.7 10.0 %collective-permute-start.1 = (bf16[72,1280]{1,0:T(8,128)(2,1)S(1)}, bf16[72,1280]{1,0:T(8,128)(2,1)S(1)}, u32[]{:S(2)}, u32[]{:S(2)}) collective-permute-start(bf16[72,1280]{1,0:T(8,128)(2,1)S(1)} %collective-permute-done.refs_0_.refs_7_), channel_id=1, source_target_pairs={{1,2},{2,3},{9,10},{10,11},{17,18},{18,19},{25,26},{26,27},{6,5},{... | collective-permute-start | bytes 552968 | tf_op jit(solution)/shard_map/ppermute | solution.py:296
  15.0 3.2 %copy-start = (bf16[1280,3072]{1,0:T(8,128)(2,1)S(1)}, bf16[1280,3072]{1,0:T(8,128)(2,1)}, u32[]{:S(2)}) copy-start(bf16[1280,3072]{1,0:T(8,128)(2,1)} %refs_3_.7) | copy-start | bytes 23592964
  18.3 3.2 %copy-start.1 = (bf16[1280,3072]{1,0:T(8,128)(2,1)S(1)}, bf16[1280,3072]{1,0:T(8,128)(2,1)}, u32[]{:S(2)}) copy-start(bf16[1280,3072]{1,0:T(8,128)(2,1)} %refs_3_.7) | copy-start | bytes 23592964
  22.9 15.3 %copy-start.2 = (bf16[1024,1280]{1,0:T(8,128)(2,1)S(1)}, bf16[1024,1280]{1,0:T(8,128)(2,1)}, u32[]{:S(2)}) copy-start(bf16[1024,1280]{1,0:T(8,128)(2,1)} %refs_10_.1) | copy-start | bytes 7864324
  22.9 6.3 %collective-permute-start.8 = (bf16[1120,128]{1,0:T(8,128)(2,1)S(1)}, bf16[1120,128]{1,0:T(8,128)(2,1)S(1)}, u32[]{:S(2)}, u32[]{:S(2)}) collective-permute-start(bf16[1120,128]{1,0:T(8,128)(2,1)S(1)} %get-tuple-element.41), channel_id=1, source_target_pairs={{5,6},{13,14},{21,22},{29,30}} | collective-permute-start | bytes 860168 | tf_op jit(solution)/shard_map/ppermute | solution.py:296
  26.0 12.2 %collective-permute-start.9 = (bf16[1120,128]{1,0:T(8,128)(2,1)S(1)}, bf16[1120,128]{1,0:T(8,128)(2,1)S(1)}, u32[]{:S(2)}, u32[]{:S(2)}) collective-permute-start(bf16[1120,128]{1,0:T(8,128)(2,1)S(1)} %get-tuple-element.47), channel_id=1, source_target_pairs={{5,7},{13,15},{21,23},{29,31}} | collective-permute-start | bytes 860168 | tf_op jit(solution)/shard_map/ppermute | solution.py:296
  26.6 11.5 %collective-permute-start.2 = (bf16[72,1280]{1,0:T(8,128)(2,1)S(1)}, bf16[72,1280]{1,0:T(8,128)(2,1)S(1)}, u32[]{:S(2)}, u32[]{:S(2)}) collective-permute-start(bf16[72,1280]{1,0:T(8,128)(2,1)S(1)} %collective-permute-done.1.refs_0_), channel_id=1, source_target_pairs={{2,3},{10,11},{18,19},{26,27}} | collective-permute-start | bytes 552968 | tf_op jit(solution)/shard_map/ppermute | solution.py:296
  27.9 10.2 %collective-permute-start.5 = (bf16[64,1280]{1,0:T(8,128)(2,1)S(1)}, bf16[64,1280]{1,0:T(8,128)(2,1)S(1)}, u32[]{:S(2)}, u32[]{:S(2)}) collective-permute-start(bf16[64,1280]{1,0:T(8,128)(2,1)S(1)} %collective-permute-done.4.refs_1_), channel_id=1, source_target_pairs={{2,3},{10,11},{18,19},{26,27}} | collective-permute-start | bytes 491528 | tf_op jit(solution)/shard_map/ppermute | solution.py:296

commit v3 on v2

v3 whole, which is shorter than its diff:
```python
import functools
import math

import jax
import jax.numpy as jnp
from jax import lax
from jax.experimental import pallas as pl
from jax.experimental.pallas import tpu as pltpu
from jax.sharding import PartitionSpec as P

HEADS = 16
PAIR = 2
LINES = HEADS // PAIR
TILE = 8
MASKED = -1e30
VMEM = pltpu.VMEM
HBM = pltpu.HBM
F32 = jnp.float32
BF16 = jnp.bfloat16
LIMIT = 20 * 1024 * 1024


def shape(dims, dtype):
    return jax.ShapeDtypeStruct(dims, dtype)


def call(body, outs, args, cost, scratch=(), aliases=None, spaces=None):
    spaces = spaces or [VMEM] * len(args)
    args = [
        pltpu.with_memory_space_constraint(a, s) if s is HBM else a for a, s in zip(args, spaces)
    ]
    return pl.pallas_call(
        body,
        out_shape=outs,
        in_specs=[pl.BlockSpec(memory_space=s) for s in spaces],
        out_specs=jax.tree.map(lambda _: pl.BlockSpec(memory_space=VMEM), outs),
        scratch_shapes=list(scratch),
        input_output_aliases=aliases or {},
        compiler_params=pltpu.CompilerParams(vmem_limit_bytes=LIMIT),
        cost_estimate=pl.CostEstimate(flops=cost, bytes_accessed=cost // 300, transcendentals=0),
    )(*args)


def plans(size):
    result = []
    for pivot in (size // 2, size // 2 - 1):
        shifts = max(pivot, size - 2 - pivot)
        slots = [("fold", t) for t in range(shifts, 0, -1)]
        slots += [("serve", t) for t in range(1, size - pivot)]
        result.append((pivot, slots))
    return result


def slot_pairs(size, pivot, slot):
    kind, t = slot
    if kind == "serve":
        return [(pivot + t, pivot)]
    return [(i, i + t) for i in range(size - t) if i + t <= pivot or i > pivot]


def receives(size, pivot, slot, place):
    kind, t = slot
    if kind == "serve":
        return place == pivot
    return ((place >= t) & (place <= pivot)) | (place > pivot + t)


def embed_body(states, kinds, episode, table, out, s_in, k_in, e_in, t_in, sems):
    ends = (states, s_in), (kinds, k_in), (episode, e_in), (table, t_in)
    copies = [pltpu.make_async_copy(*end, sems.at[k]) for k, end in enumerate(ends)]
    for copy in copies:
        copy.start()
    for copy in copies[::-1]:
        copy.wait()
    rows, width = states.shape
    count = table.shape[0]
    numbers = lax.broadcasted_iota(jnp.int32, (count, rows), 0)
    picked = (numbers == k_in[...]).astype(BF16)
    added = lax.dot_general(
        picked, t_in[...], (((0,), (0,)), ((), ())), preferred_element_type=F32
    )
    out[:rows, :] = (s_in[...].astype(F32) + added).astype(BF16)
    out[rows:, :] = jnp.zeros((TILE, width), BF16)
    out[rows:, :rows] = jnp.broadcast_to(e_in[...].astype(F32), (TILE, rows)).astype(BF16)


def episode_of(block):
    rows = block.shape[0] - TILE
    return block[rows : rows + 1, :rows].astype(F32)


def same_episode(key_block, query_block):
    keys, queries = episode_of(key_block), episode_of(query_block)
    return jnp.broadcast_to(keys, (queries.shape[1], keys.shape[1])).T == queries


def fold(first, mask, keys, values_t, wide_q, top, total, acc, factor):
    rows = mask.shape[1]
    head = wide_q.shape[0] // HEADS
    wide_mask = jnp.concatenate([mask] * PAIR, axis=1)
    for pair in range(LINES):
        span = slice(pair * PAIR * head, (pair + 1) * PAIR * head)
        scores = jnp.dot(keys[:, span], wide_q[span, :], preferred_element_type=F32)
        scores = jnp.where(wide_mask, scores, MASKED)
        here = jnp.max(scores, axis=0, keepdims=True)
        line = slice(pair, pair + 1)
        if first:
            raised = here
        else:
            before = top[line, :]
            raised = jnp.maximum(before, here)
            shrink = jnp.exp2((before - raised) * factor)
        weights = jnp.exp2((scores - raised) * factor)
        added = jnp.sum(weights, axis=0, keepdims=True)
        top[line, :] = raised
        total[line, :] = added if first else total[line, :] * shrink + added
        summed = jnp.dot(values_t[span, :], weights.astype(BF16), preferred_element_type=F32)
        for one in range(PAIR):
            place = slice(span.start + one * head, span.start + (one + 1) * head)
            lanes = slice(one * rows, (one + 1) * rows)
            part = summed[one * head : (one + 1) * head, lanes]
            acc[place, :] = part if first else acc[place, :] * shrink[:, lanes] + part


def inputs_of(block):
    return block[: block.shape[0] - TILE, :]


def put_keys_values(x, w, keys, values_t):
    inner = w.shape[1] // 3
    keys[...] = jnp.dot(x, w[:, inner : 2 * inner], preferred_element_type=F32).astype(BF16)
    values = jnp.dot(x, w[:, 2 * inner :], preferred_element_type=F32)
    values_t[...] = values.astype(BF16).T


def put_queries(x, w, wide_q):
    inner = w.shape[1] // 3
    head = inner // HEADS
    queries = jnp.dot(x, w[:, :inner], preferred_element_type=F32).astype(BF16).T
    empty = jnp.zeros((head, x.shape[0]), BF16)
    for number in range(HEADS):
        one = number % PAIR
        place = slice(number * head, (number + 1) * head)
        parts = [queries[place, :] if k == one else empty for k in range(PAIR)]
        wide_q[place, :] = jnp.concatenate(parts, axis=1)


def own_body(factor, block, w_qkv, w, keys, values_t, wide_q, top, total, acc, sems):
    inner = w_qkv.shape[1] // 3
    copies = []
    for k in range(3):
        part = (slice(None), slice(k * inner, (k + 1) * inner))
        copies.append(pltpu.make_async_copy(w_qkv.at[part], w.at[part], sems.at[k]))
        copies[k].start()
    x = inputs_of(block)
    rows = x.shape[0]
    copies[0].wait()
    put_queries(x, w, wide_q)
    copies[1].wait()
    copies[2].wait()
    put_keys_values(x, w, keys, values_t)
    place_k = lax.broadcasted_iota(jnp.int32, (rows, rows), 0)
    place_q = lax.broadcasted_iota(jnp.int32, (rows, rows), 1)
    mask = (place_k <= place_q) & same_episode(block, block)
    fold(True, mask, keys, values_t, wide_q, top, total, acc, factor)


def split_three(value):
    high = value.astype(BF16)
    rest = value - high.astype(F32)
    middle = rest.astype(BF16)
    low = (rest - middle.astype(F32)).astype(BF16)
    return [high, middle, low]


def pack(top, total, acc, out):
    inner, rows = acc.shape
    head = inner // HEADS
    scale = 1.0 / total[...]
    for number in range(HEADS):
        pair, one = divmod(number, PAIR)
        place = slice(number * head, (number + 1) * head)
        lanes = slice(one * rows, (one + 1) * rows)
        out[place, :] = (acc[place, :] * scale[pair : pair + 1, lanes]).astype(BF16)
    parts = []
    for value in (top[...], total[...]):
        lanes = [value[:, k * rows : (k + 1) * rows] for k in range(PAIR)]
        parts += split_three(jnp.concatenate(lanes, axis=0))
    for number, part in enumerate(parts):
        out[inner + number * HEADS : inner + (number + 1) * HEADS, :] = part


def merge(packed, top, total, acc, factor):
    inner, rows = acc.shape
    head = inner // HEADS

    def read(number):
        start = inner + number * 3 * HEADS
        parts = [
            packed[start + k * HEADS : start + (k + 1) * HEADS, :].astype(F32) for k in range(3)
        ]
        whole = (parts[0] + parts[1]) + parts[2]
        return jnp.concatenate([whole[k * LINES : (k + 1) * LINES] for k in range(PAIR)], axis=1)

    other_top, other_total = read(0), read(1)
    before = top[...]
    raised = jnp.maximum(before, other_top)
    shrink = jnp.exp2((before - raised) * factor)
    weight = jnp.exp2((other_top - raised) * factor) * other_total
    top[...] = raised
    total[...] = total[...] * shrink + weight
    for number in range(HEADS):
        pair, one = divmod(number, PAIR)
        place = slice(number * head, (number + 1) * head)
        line, lanes = slice(pair, pair + 1), slice(one * rows, (one + 1) * rows)
        acc[place, :] = (
            acc[place, :] * shrink[line, lanes] + packed[place, :].astype(F32) * weight[line, lanes]
        )


def slot_body(size, jobs, kept_at, count, factor, folds, serves, *refs):
    refs = list(refs)
    take = lambda count: [refs.pop(0) for _ in range(count)]
    block, mine, w, wide_q = take(4)
    blocks, kept = take(count), take(2 * count)
    take(3)
    top, total, acc = take(3)
    keys, values_t = take(2) if folds else (None, None)
    packed = take(1)[0] if serves else None
    place = lax.axis_index("seq")
    parity = lax.rem(lax.axis_index("dp"), 2)
    for number, (pivot, slot) in enumerate(jobs):
        if slot is None:
            continue

        @pl.when((parity == number) & receives(size, pivot, slot, place))
        def _(kind=slot[0], numbers=kept_at[number]):
            x = inputs_of(block)
            if kind == "fold":
                put_keys_values(x, w, keys, values_t)
                mask = same_episode(block, mine)
                fold(False, mask, keys, values_t, wide_q, top, total, acc, factor)
            else:
                other_q, *state = refs
                put_queries(x, w, other_q)
                for order, k in enumerate(numbers):
                    mask = same_episode(blocks[k], block)
                    pair = kept[2 * k : 2 * k + 2]
                    fold(order == 0, mask, *pair, other_q, *state, factor)
                pack(*state, packed)


def last_body(targets, factor, *refs):
    count = len(targets)
    packed = refs[:count]
    top_in, total_in, acc_in, w_out, out, top, total, acc = refs[count:]
    place = lax.axis_index("seq")
    parity = lax.rem(lax.axis_index("dp"), 2)
    top[...] = top_in[...]
    total[...] = total_in[...]
    acc[...] = acc_in[...]
    for part, places in zip(packed, targets):
        for number, where in enumerate(places):
            if where is not None:

                @pl.when((parity == number) & (place == where))
                def _(part=part):
                    merge(part, top, total, acc, factor)

    inner, rows = acc.shape
    head = inner // HEADS
    parts = []
    for number in range(HEADS):
        pair, one = divmod(number, PAIR)
        scale = 1.0 / total[pair : pair + 1, one * rows : (one + 1) * rows]
        parts.append((acc[number * head : (number + 1) * head, :] * scale).astype(BF16))
    heads_out = jnp.concatenate(parts, axis=0).T
    out[...] = jnp.dot(heads_out, w_out[...], preferred_element_type=F32).astype(out.dtype)


def local(groups, size, states, token_kind, episode, kind_table, w_qkv, w_out):
    rows, width = states.shape
    inner = w_out.shape[0]
    head = inner // HEADS
    factor = math.log2(math.e) / math.sqrt(head)
    kinds = plans(size)
    slots = max(len(s) for _, s in kinds)

    def move(value, pairs_by_parity):
        pairs = []
        for group in range(groups):
            pairs += [(group * size + a, group * size + b) for a, b in pairs_by_parity[group % 2]]
        return lax.ppermute(value, ("dp", "seq"), pairs)

    unit = 2 * rows * width * inner
    args = (states, token_kind.reshape(1, rows), episode.reshape(1, rows), kind_table)
    mine = call(
        embed_body,
        shape((rows + TILE, width), BF16),
        args,
        unit,
        [VMEM(a.shape, a.dtype) for a in args] + [pltpu.SemaphoreType.DMA((len(args),))],
        spaces=[HBM] * len(args),
    )
    jobs = [[(p, s[k] if k < len(s) else None) for p, s in kinds] for k in range(slots)]
    moving = []
    for job in jobs:
        moving.append(move(mine, [slot_pairs(size, p, s) if s else [] for p, s in job]))

    state = [
        shape((LINES, PAIR * rows), F32),
        shape((LINES, PAIR * rows), F32),
        shape((inner, rows), F32),
    ]
    wide = shape((inner, PAIR * rows), BF16)
    pair = [shape((rows, inner), BF16), shape((inner, rows), BF16)]
    w, keys, values_t, wide_q, *now = call(
        functools.partial(own_body, factor),
        [shape(w_qkv.shape, w_qkv.dtype)] + pair + [wide] + state,
        (mine, w_qkv),
        3 * unit,
        [pltpu.SemaphoreType.DMA((3,))],
        spaces=[VMEM, HBM],
    )
    blocks, kept, kept_at = [mine], [keys, values_t], [[0], [0]]
    returned, targets = [], []
    for job, block in zip(jobs, moving):
        folds = any(s and s[0] == "fold" for _, s in job)
        serves = any(s and s[0] == "serve" for _, s in job)
        args = (block, mine, w, wide_q, *blocks, *kept, *now)
        outs = state + (pair if folds else [])
        outs += [shape((inner + 6 * HEADS, rows), BF16)] if serves else []
        got = call(
            functools.partial(
                slot_body, size, job, [list(k) for k in kept_at], len(blocks), factor, folds, serves
            ),
            outs,
            args,
            2 * unit,
            [VMEM(s.shape, s.dtype) for s in [wide] + state],
            {len(args) - 3 + k: k for k in range(3)},
        )
        now = got[:3]
        if serves:
            chosen = [(p, s[1]) if s and s[0] == "serve" else None for p, s in job]
            returned.append(move(got[-1], [[(c[0], sum(c))] if c else [] for c in chosen]))
            targets.append([sum(c) if c else None for c in chosen])
        if folds:
            for number, (pivot, slot) in enumerate(job):
                if slot and slot[0] == "fold" and slot[1] <= pivot:
                    kept_at[number].append(len(blocks))
            blocks, kept = blocks + [block], kept + list(got[3:5])
    args = (*returned, *now, w_out)
    return call(
        functools.partial(last_body, targets, factor),
        shape((rows, w_out.shape[1]), BF16),
        args,
        2 * unit,
        [VMEM(s.shape, s.dtype) for s in state],
    )


def solution(mesh):
    placed = (P(("dp", "seq"), None), P(("dp", "seq")), P(("dp", "seq")), P(), P(), P())
    return jax.shard_map(
        functools.partial(local, mesh.shape["dp"], mesh.shape["seq"]),
        mesh=mesh,
        in_specs=placed,
        out_specs=P(("dp", "seq"), None),
        check_vma=False,
    )
```

time: 41.3 us -> 30.4 us (0.74)
  local copies, waits for them, and re-layouts: 7.68 us -> 0.01 us
  starting transfers between devices: 10.6 us -> 7.05 us
  waiting for transfers between devices: 14.2 us -> 15.5 us
  Pallas kernels: 8.31 us -> 7.48 us
    unnamed x14 -> x2, local copies, waits for them, and re-layouts: 7.68 us -> 0.01 us
    ppermute x10 -> x5, starting transfers between devices: 10.6 us -> 7.05 us  [move(): return lax.ppermute(value, ('dp', 'seq'), pairs)]
    ppermute x10 -> x5, waiting for transfers between devices: 14.2 us -> 15.5 us  [move(): return lax.ppermute(value, ('dp', 'seq'), pairs)]
    pallas_call x6, Pallas kernels: 8.31 us -> 7.48 us  [call(): pl.pallas_call(body, out_shape=outs, in_specs=[pl.BlockSpec(memory_space=...]
  transfers between devices with their start and end apart: 10 -> 5, of which waited for: 2 -> 2; matrix products, arithmetic and copies ran while one was open for 0% -> 0% of each run, Pallas kernels for 13% -> 16%
where the time goes in v3:
time: 30.4 us; the launch traced here: 30.2 us
  waiting for transfers between devices  15.5 us (51%)
  Pallas kernels  7.48 us (25%)
  starting transfers between devices  7.05 us (23%)
    ppermute x5, waiting for transfers between devices, move(): return lax.ppermute(value, ('dp', 'seq'), pairs)  15.5 us
    pallas_call x6, Pallas kernels, call(): pl.pallas_call(body, out_shape=outs, in_specs=[pl.BlockSpec(memory_space=...  7.48 us
    ppermute x5, starting transfers between devices, move(): return lax.ppermute(value, ('dp', 'seq'), pairs)  7.05 us
  transfers between devices with their start and end apart: 5, of which 2 were waited for; matrix products, arithmetic and copies ran while one was open for 0% of the time, Pallas kernels for 16%

profile of v3, /device:TPU:30, one launch (start us, length us, event | category | flops | bytes accessed | tf_op | source)
XLA Modules:
  0.0 30.2 jit_solution(6036347942459890891)
XLA Ops:
  0.0 1.3 %shard_map.64.block.refs_1_.refs_4_ = bf16[136,1280]{1,0:T(8,128)(2,1)S(1)} custom-call(bf16[128,1280]{1,0:T(8,128)(2,1)} %states.1, s32[1,128]{1,0:T(1,128)} %bitcast.2, s32[1,128]{1,0:T(1,128)} %bitcast.3, bf16[4,1280]{1,0:T(4,128)(2,1)} %table.1), custom_call_target="tpu_custom_call" | custom-call | flops 335544320 | bytes 1118481 | tf_op jit(solution)/shard_map/pallas_call | solution.py:32
  1.3 0.7 %collective-permute-start.1 = (bf16[136,1280]{1,0:T(8,128)(2,1)S(1)}, bf16[136,1280]{1,0:T(8,128)(2,1)S(1)}, u32[]{:S(2)}, u32[]{:S(2)}) collective-permute-start(bf16[136,1280]{1,0:T(8,128)(2,1)S(1)} %shard_map.64.block.refs_1_.refs_4_), channel_id=1, source_target_pairs={{0,2},{4,5},{6,7},{8,10},{12,13},{14,15},{16,18},{20,21},{22,23},{... | collective-permute-start | bytes 1044488 | tf_op jit(solution)/shard_map/ppermute | solution.py:293
  2.0 0.7 %collective-permute-start = (bf16[136,1280]{1,0:T(8,128)(2,1)S(1)}, bf16[136,1280]{1,0:T(8,128)(2,1)S(1)}, u32[]{:S(2)}, u32[]{:S(2)}) collective-permute-start(bf16[136,1280]{1,0:T(8,128)(2,1)S(1)} %shard_map.64.block.refs_1_.refs_4_), channel_id=1, source_target_pairs={{0,1},{1,2},{6,5},{8,9},{9,10},{14,13},{16,17},{17,18},{22,21},{24... | collective-permute-start | bytes 1044488 | tf_op jit(solution)/shard_map/ppermute | solution.py:293
  2.7 3.6 %collective-permute-start.3 = (bf16[136,1280]{1,0:T(8,128)(2,1)S(1)}, bf16[136,1280]{1,0:T(8,128)(2,1)S(1)}, u32[]{:S(2)}, u32[]{:S(2)}) collective-permute-start(bf16[136,1280]{1,0:T(8,128)(2,1)S(1)} %shard_map.64.block.refs_1_.refs_4_), channel_id=1, source_target_pairs={{3,2},{7,5},{11,10},{15,13},{19,18},{23,21},{27,26},{31,29}} | collective-permute-start | bytes 1044488 | tf_op jit(solution)/shard_map/ppermute | solution.py:293
  6.3 4.7 %shard_map.65 = (bf16[1280,3072]{1,0:T(8,128)(2,1)S(1)}, bf16[128,1024]{1,0:T(8,128)(2,1)S(1)}, bf16[1024,128]{1,0:T(8,128)(2,1)S(1)}, bf16[1024,256]{1,0:T(8,12...) custom-call(bf16[136,1280]{1,0:T(8,128)(2,1)S(1)} %shard_map.64.block.refs_1_.refs_4_, ...), custom_call_target="tpu_custom_call" | custom-call | flops 1006632960 | bytes 3355443 | tf_op jit(solution)/shard_map/pallas_call | solution.py:32
  11.0 0.0 collective-permute-done.1.refs_0_.refs_5_
  11.1 0.0 collective-permute-done.refs_0_.refs_6_
  11.1 0.0 copy-start
  11.1 0.8 %collective-permute-start.2 = (bf16[1120,128]{1,0:T(8,128)(2,1)S(1)}, bf16[1120,128]{1,0:T(8,128)(2,1)S(1)}, u32[]{:S(2)}, u32[]{:S(2)}) collective-permute-start(bf16[1120,128]{1,0:T(8,128)(2,1)S(1)} %get-tuple-element.39), channel_id=1, source_target_pairs={{5,6},{13,14},{21,22},{29,30}} | collective-permute-start | bytes 860168 | tf_op jit(solution)/shard_map/ppermute | solution.py:293
  11.9 1.6 %collective-permute-done.3.refs_0_ = bf16[136,1280]{1,0:T(8,128)(2,1)S(1)} collective-permute-done((bf16[136,1280]{1,0:T(8,128)(2,1)S(1)}, bf16[136,1280]{1,0:T(8,128)(2,1)S(1)}, u32[]{:S(2)}, u32[]{:S(2)}) %collective-permute-start.3) | collective-permute-done | bytes 348192 | tf_op jit(solution)/shard_map/ppermute | solution.py:293
  13.6 1.3 %collective-permute-start.4 = (bf16[1120,128]{1,0:T(8,128)(2,1)S(1)}, bf16[1120,128]{1,0:T(8,128)(2,1)S(1)}, u32[]{:S(2)}, u32[]{:S(2)}) collective-permute-start(bf16[1120,128]{1,0:T(8,128)(2,1)S(1)} %get-tuple-element.45), channel_id=1, source_target_pairs={{2,3},{5,7},{10,11},{13,15},{18,19},{21,23},{26,27},{29,31}} | collective-permute-start | bytes 860168 | tf_op jit(solution)/shard_map/ppermute | solution.py:293
  14.9 0.0 collective-permute-done.2.refs_0_
  14.9 13.9 %collective-permute-done.4.refs_1_ = bf16[1120,128]{1,0:T(8,128)(2,1)S(1)} collective-permute-done((bf16[1120,128]{1,0:T(8,128)(2,1)S(1)}, bf16[1120,128]{1,0:T(8,128)(2,1)S(1)}, u32[]{:S(2)}, u32[]{:S(2)}) %collective-permute-start.4) | collective-permute-done | bytes 286752 | tf_op jit(solution)/shard_map/ppermute | solution.py:293
  28.8 0.0 copy-done
  28.8 1.4 %shard_map.69 = bf16[128,1280]{1,0:T(8,128)(2,1)} custom-call(bf16[1120,128]{1,0:T(8,128)(2,1)S(1)} %collective-permute-done.2.refs_0_, bf16[1120,128]{1,0:T(8,128)(2,1)S(1)} %collective-permute-done.4.refs_1_, f32[8,256]{1,0:T(8,128)S(1)} %get-tuple-element.46.refs_2_, f32[8,256]{1,0:T(8,128)S(1)} %get-tuple-element.47.refs_3_, ...), custom_call_target="tpu_custom_call" | custom-call | flops 671088640 | bytes 2236962 | tf_op jit(solution)/shard_map/pallas_call | solution.py:32
  (3 shorter events, 0.1 us)
Async XLA Ops:
  1.3 9.7 %collective-permute-start.1 = (bf16[136,1280]{1,0:T(8,128)(2,1)S(1)}, bf16[136,1280]{1,0:T(8,128)(2,1)S(1)}, u32[]{:S(2)}, u32[]{:S(2)}) collective-permute-start(bf16[136,1280]{1,0:T(8,128)(2,1)S(1)} %shard_map.64.block.refs_1_.refs_4_), channel_id=1, source_target_pairs={{0,2},{4,5},{6,7},{8,10},{12,13},{14,15},{16,18},{20,21},{22,23},{... | collective-permute-start | bytes 1044488 | tf_op jit(solution)/shard_map/ppermute | solution.py:293
  2.0 9.1 %collective-permute-start = (bf16[136,1280]{1,0:T(8,128)(2,1)S(1)}, bf16[136,1280]{1,0:T(8,128)(2,1)S(1)}, u32[]{:S(2)}, u32[]{:S(2)}) collective-permute-start(bf16[136,1280]{1,0:T(8,128)(2,1)S(1)} %shard_map.64.block.refs_1_.refs_4_), channel_id=1, source_target_pairs={{0,1},{1,2},{6,5},{8,9},{9,10},{14,13},{16,17},{17,18},{22,21},{24... | collective-permute-start | bytes 1044488 | tf_op jit(solution)/shard_map/ppermute | solution.py:293
  2.7 10.9 %collective-permute-start.3 = (bf16[136,1280]{1,0:T(8,128)(2,1)S(1)}, bf16[136,1280]{1,0:T(8,128)(2,1)S(1)}, u32[]{:S(2)}, u32[]{:S(2)}) collective-permute-start(bf16[136,1280]{1,0:T(8,128)(2,1)S(1)} %shard_map.64.block.refs_1_.refs_4_), channel_id=1, source_target_pairs={{3,2},{7,5},{11,10},{15,13},{19,18},{23,21},{27,26},{31,29}} | collective-permute-start | bytes 1044488 | tf_op jit(solution)/shard_map/ppermute | solution.py:293
  11.1 17.7 %copy-start = (bf16[1024,1280]{1,0:T(8,128)(2,1)S(1)}, bf16[1024,1280]{1,0:T(8,128)(2,1)}, u32[]{:S(2)}) copy-start(bf16[1024,1280]{1,0:T(8,128)(2,1)} %refs_5_.1) | copy-start | bytes 7864324
  11.1 3.8 %collective-permute-start.2 = (bf16[1120,128]{1,0:T(8,128)(2,1)S(1)}, bf16[1120,128]{1,0:T(8,128)(2,1)S(1)}, u32[]{:S(2)}, u32[]{:S(2)}) collective-permute-start(bf16[1120,128]{1,0:T(8,128)(2,1)S(1)} %get-tuple-element.39), channel_id=1, source_target_pairs={{5,6},{13,14},{21,22},{29,30}} | collective-permute-start | bytes 860168 | tf_op jit(solution)/shard_map/ppermute | solution.py:293
  13.6 15.2 %collective-permute-start.4 = (bf16[1120,128]{1,0:T(8,128)(2,1)S(1)}, bf16[1120,128]{1,0:T(8,128)(2,1)S(1)}, u32[]{:S(2)}, u32[]{:S(2)}) collective-permute-start(bf16[1120,128]{1,0:T(8,128)(2,1)S(1)} %get-tuple-element.45), channel_id=1, source_target_pairs={{2,3},{5,7},{10,11},{13,15},{18,19},{21,23},{26,27},{29,31}} | collective-permute-start | bytes 860168 | tf_op jit(solution)/shard_map/ppermute | solution.py:293

commit v4 on v3

--- a/solution.py
+++ b/solution.py
@@ -12,6 +12,7 @@
 PAIR = 2
 LINES = HEADS // PAIR
 TILE = 8
+SPLIT = 2
 MASKED = -1e30
 VMEM = pltpu.VMEM
 HBM = pltpu.HBM
@@ -41,28 +42,19 @@
     )(*args)
 
 
-def plans(size):
-    result = []
-    for pivot in (size // 2, size // 2 - 1):
-        shifts = max(pivot, size - 2 - pivot)
-        slots = [("fold", t) for t in range(shifts, 0, -1)]
-        slots += [("serve", t) for t in range(1, size - pivot)]
-        result.append((pivot, slots))
-    return result
-
-
-def slot_pairs(size, pivot, slot):
-    kind, t = slot
-    if kind == "serve":
-        return [(pivot + t, pivot)]
-    return [(i, i + t) for i in range(size - t) if i + t <= pivot or i > pivot]
-
-
-def receives(size, pivot, slot, place):
-    kind, t = slot
-    if kind == "serve":
-        return place == pivot
-    return ((place >= t) & (place <= pivot)) | (place > pivot + t)
+def plan_of(size, pivot):
+    sources = list(range(pivot - 1, -1, -1)) + list(range(size - 1, pivot, -1))
+    slots = [[(source, pivot)] for source in sources]
+    for i in range(size):
+        for j in range(i):
+            if i != pivot and (i < pivot or j > pivot):
+                free = [s for s in slots if all(j != a and i != b for a, b in s)]
+                if free:
+                    free[-1].append((j, i))
+                else:
+                    slots.append([(j, i)])
+    sources += [None] * (len(slots) - len(sources))
+    return sources, slots
 
 
 def embed_body(states, kinds, episode, table, out, s_in, k_in, e_in, t_in, sems):
@@ -147,17 +139,21 @@
 
 def own_body(factor, block, w_qkv, w, keys, values_t, wide_q, top, total, acc, sems):
     inner = w_qkv.shape[1] // 3
+    depth = w_qkv.shape[0] // SPLIT
     copies = []
     for k in range(3):
-        part = (slice(None), slice(k * inner, (k + 1) * inner))
-        copies.append(pltpu.make_async_copy(w_qkv.at[part], w.at[part], sems.at[k]))
-        copies[k].start()
+        for r in range(SPLIT):
+            part = (slice(r * depth, (r + 1) * depth), slice(k * inner, (k + 1) * inner))
+            sem = sems.at[k * SPLIT + r]
+            copies.append(pltpu.make_async_copy(w_qkv.at[part], w.at[part], sem))
+            copies[-1].start()
     x = inputs_of(block)
     rows = x.shape[0]
-    copies[0].wait()
+    for copy in copies[:SPLIT]:
+        copy.wait()
     put_queries(x, w, wide_q)
-    copies[1].wait()
-    copies[2].wait()
+    for copy in copies[SPLIT:]:
+        copy.wait()
     put_keys_values(x, w, keys, values_t)
     place_k = lax.broadcasted_iota(jnp.int32, (rows, rows), 0)
     place_q = lax.broadcasted_iota(jnp.int32, (rows, rows), 1)
@@ -218,7 +214,14 @@
         )
 
 
-def slot_body(size, jobs, kept_at, count, factor, folds, serves, *refs):
+def any_of(place, places):
+    found = place < 0
+    for one in places:
+        found = found | (place == one)
+    return found
+
+
+def slot_body(jobs, kept_at, count, factor, folds, serves, *refs):
     refs = list(refs)
     take = lambda count: [refs.pop(0) for _ in range(count)]
     block, mine, w, wide_q = take(4)
@@ -229,20 +232,28 @@
     packed = take(1)[0] if serves else None
     place = lax.axis_index("seq")
     parity = lax.rem(lax.axis_index("dp"), 2)
-    for number, (pivot, slot) in enumerate(jobs):
-        if slot is None:
-            continue
-
-        @pl.when((parity == number) & receives(size, pivot, slot, place))
-        def _(kind=slot[0], numbers=kept_at[number]):
-            x = inputs_of(block)
-            if kind == "fold":
-                put_keys_values(x, w, keys, values_t)
+    for number, (pivot, source, pairs) in enumerate(jobs):
+        here = parity == number
+        others = [b for _, b in pairs if b != pivot]
+
+        if others:
+
+            @pl.when(here & any_of(place, others))
+            def _():
+                put_keys_values(inputs_of(block), w, keys, values_t)
                 mask = same_episode(block, mine)
                 fold(False, mask, keys, values_t, wide_q, top, total, acc, factor)
+
+        if source is None:
+            continue
+
+        @pl.when(here & (place == pivot))
+        def _(pivot=pivot, source=source, numbers=kept_at[number]):
+            if source < pivot:
+                put_keys_values(inputs_of(block), w, keys, values_t)
             else:
                 other_q, *state = refs
-                put_queries(x, w, other_q)
+                put_queries(inputs_of(block), w, other_q)
                 for order, k in enumerate(numbers):
                     mask = same_episode(blocks[k], block)
                     pair = kept[2 * k : 2 * k + 2]
@@ -250,15 +261,26 @@
                 pack(*state, packed)
 
 
-def last_body(targets, factor, *refs):
-    count = len(targets)
-    packed = refs[:count]
-    top_in, total_in, acc_in, w_out, out, top, total, acc = refs[count:]
+def last_body(targets, pivots, kept_at, count, factor, *refs):
+    refs = list(refs)
+    take = lambda count: [refs.pop(0) for _ in range(count)]
+    mine, wide_q = take(2)
+    blocks, kept, packed = take(count), take(2 * count), take(len(targets))
+    top_in, total_in, acc_in, w_out, out, top, total, acc = refs
     place = lax.axis_index("seq")
     parity = lax.rem(lax.axis_index("dp"), 2)
     top[...] = top_in[...]
     total[...] = total_in[...]
     acc[...] = acc_in[...]
+    for number, pivot in enumerate(pivots):
+
+        @pl.when((parity == number) & (place == pivot))
+        def _(numbers=kept_at[number]):
+            for k in numbers[1:]:
+                mask = same_episode(blocks[k], mine)
+                pair = kept[2 * k : 2 * k + 2]
+                fold(False, mask, *pair, wide_q, top, total, acc, factor)
+
     for part, places in zip(packed, targets):
         for number, where in enumerate(places):
             if where is not None:
@@ -283,8 +305,9 @@
     inner = w_out.shape[0]
     head = inner // HEADS
     factor = math.log2(math.e) / math.sqrt(head)
-    kinds = plans(size)
-    slots = max(len(s) for _, s in kinds)
+    pivots = (size // 2, size // 2 - 1)
+    kinds = [plan_of(size, pivot) for pivot in pivots]
+    count = max(len(sources) for sources, _ in kinds)
 
     def move(value, pairs_by_parity):
         pairs = []
@@ -302,10 +325,13 @@
         [VMEM(a.shape, a.dtype) for a in args] + [pltpu.SemaphoreType.DMA((len(args),))],
         spaces=[HBM] * len(args),
     )
-    jobs = [[(p, s[k] if k < len(s) else None) for p, s in kinds] for k in range(slots)]
-    moving = []
-    for job in jobs:
-        moving.append(move(mine, [slot_pairs(size, p, s) if s else [] for p, s in job]))
+    jobs = []
+    for k in range(count):
+        job = []
+        for pivot, (sources, slots) in zip(pivots, kinds):
+            job.append((pivot, sources[k], slots[k]) if k < len(slots) else (pivot, None, []))
+        jobs.append(job)
+    moving = [move(mine, [pairs for _, _, pairs in job]) for job in jobs]
 
     state = [
         shape((LINES, PAIR * rows), F32),
@@ -319,21 +345,22 @@
         [shape(w_qkv.shape, w_qkv.dtype)] + pair + [wide] + state,
         (mine, w_qkv),
         3 * unit,
-        [pltpu.SemaphoreType.DMA((3,))],
+        [pltpu.SemaphoreType.DMA((3 * SPLIT,))],
         spaces=[VMEM, HBM],
     )
     blocks, kept, kept_at = [mine], [keys, values_t], [[0], [0]]
     returned, targets = [], []
     for job, block in zip(jobs, moving):
-        folds = any(s and s[0] == "fold" for _, s in job)
-        serves = any(s and s[0] == "serve" for _, s in job)
+        serve = [s if s is not None and s > p else None for p, s, _ in job]
+        keep = [s is not None and s < p for p, s, _ in job]
+        serves = any(s is not None for s in serve)
+        folds = any(keep) or any(b != p for p, _, pairs in job for _, b in pairs)
         args = (block, mine, w, wide_q, *blocks, *kept, *now)
         outs = state + (pair if folds else [])
         outs += [shape((inner + 6 * HEADS, rows), BF16)] if serves else []
+        numbers = [list(k) for k in kept_at]
         got = call(
-            functools.partial(
-                slot_body, size, job, [list(k) for k in kept_at], len(blocks), factor, folds, serves
-            ),
+            functools.partial(slot_body, job, numbers, len(blocks), factor, folds, serves),
             outs,
             args,
             2 * unit,
@@ -342,17 +369,17 @@
         )
         now = got[:3]
         if serves:
-            chosen = [(p, s[1]) if s and s[0] == "serve" else None for p, s in job]
-            returned.append(move(got[-1], [[(c[0], sum(c))] if c else [] for c in chosen]))
-            targets.append([sum(c) if c else None for c in chosen])
-        if folds:
-            for number, (pivot, slot) in enumerate(job):
-                if slot and slot[0] == "fold" and slot[1] <= pivot:
+            pairs = [[] if s is None else [(p, s)] for p, s in zip(pivots, serve)]
+            returned.append(move(got[-1], pairs))
+            targets.append(serve)
+        if any(keep):
+            for number in range(len(pivots)):
+                if keep[number]:
                     kept_at[number].append(len(blocks))
             blocks, kept = blocks + [block], kept + list(got[3:5])
-    args = (*returned, *now, w_out)
+    args = (mine, wide_q, *blocks, *kept, *returned, *now, w_out)
     return call(
-        functools.partial(last_body, targets, factor),
+        functools.partial(last_body, targets, pivots, kept_at, len(blocks), factor),
         shape((rows, w_out.shape[1]), BF16),
         args,
         2 * unit,

time: 30.4 us -> 27.6 us (0.908)
  waiting for transfers between devices: 15.5 us -> 11.9 us
  Pallas kernels: 7.48 us -> 8.26 us
    ppermute x5, waiting for transfers between devices: 15.5 us -> 11.9 us  [move(): return lax.ppermute(value, ('dp', 'seq'), pairs)]
    pallas_call x6, Pallas kernels: 7.48 us -> 8.26 us  [call(): pl.pallas_call(body, out_shape=outs, in_specs=[pl.BlockSpec(memory_space=...]
  transfers between devices with their start and end apart: 5 -> 5, of which waited for: 2 -> 2; matrix products, arithmetic and copies ran while one was open for 0% -> 0% of each run, Pallas kernels for 16% -> 20%
where the time goes in v4:
time: 27.6 us; the launch traced here: 27.4 us
  waiting for transfers between devices  11.9 us (43%)
  Pallas kernels  8.26 us (30%)
  starting transfers between devices  7.05 us (26%)
    ppermute x5, waiting for transfers between devices, move(): return lax.ppermute(value, ('dp', 'seq'), pairs)  11.9 us
    pallas_call x6, Pallas kernels, call(): pl.pallas_call(body, out_shape=outs, in_specs=[pl.BlockSpec(memory_space=...  8.26 us
    ppermute x5, starting transfers between devices, move(): return lax.ppermute(value, ('dp', 'seq'), pairs)  7.05 us
  transfers between devices with their start and end apart: 5, of which 2 were waited for; matrix products, arithmetic and copies ran while one was open for 0% of the time, Pallas kernels for 20%

profile of v4, /device:TPU:30, one launch (start us, length us, event | category | flops | bytes accessed | tf_op | source)
XLA Modules:
  0.0 27.4 jit_solution(1868442788204903557)
XLA Ops:
  0.0 1.3 %shard_map.64.block.refs_1_.refs_4_.refs_0_.refs_2_ = bf16[136,1280]{1,0:T(8,128)(2,1)S(1)} custom-call(bf16[128,1280]{1,0:T(8,128)(2,1)} %states.1, s32[1,128]{1,0:T(1,128)} %bitcast.2, s32[1,128]{1,0:T(1,128)} %bitcast.3, bf16[4,1280]{1,0:T(4,128)(2,1)} %table.1), custom_call_target="tpu_custom_call" | custom-call | flops 335544320 | bytes 1118481 | tf_op jit(solution)/shard_map/pallas_call | solution.py:33
  1.3 0.7 %collective-permute-start = (bf16[136,1280]{1,0:T(8,128)(2,1)S(1)}, bf16[136,1280]{1,0:T(8,128)(2,1)S(1)}, u32[]{:S(2)}, u32[]{:S(2)}) collective-permute-start(bf16[136,1280]{1,0:T(8,128)(2,1)S(1)} %shard_map.64.block.refs_1_.refs_4_.refs_0_.refs_2_), channel_id=1, source_target_pairs={{1,2},{4,5},{9,10},{12,13},{17,18},{20,21},{25,26},{28,29}} | collective-permute-start | bytes 1044488 | tf_op jit(solution)/shard_map/ppermute | solution.py:316
  2.0 0.7 %collective-permute-start.1 = (bf16[136,1280]{1,0:T(8,128)(2,1)S(1)}, bf16[136,1280]{1,0:T(8,128)(2,1)S(1)}, u32[]{:S(2)}, u32[]{:S(2)}) collective-permute-start(bf16[136,1280]{1,0:T(8,128)(2,1)S(1)} %shard_map.64.block.refs_1_.refs_4_.refs_0_.refs_2_), channel_id=1, source_target_pairs={{0,2},{7,5},{6,7},{8,10},{15,13},{14,15},{16,18},{23,21},{22,23},{... | collective-permute-start | bytes 1044488 | tf_op jit(solution)/shard_map/ppermute | solution.py:316
  2.7 3.6 %collective-permute-start.3 = (bf16[136,1280]{1,0:T(8,128)(2,1)S(1)}, bf16[136,1280]{1,0:T(8,128)(2,1)S(1)}, u32[]{:S(2)}, u32[]{:S(2)}) collective-permute-start(bf16[136,1280]{1,0:T(8,128)(2,1)S(1)} %shard_map.64.block.refs_1_.refs_4_.refs_0_.refs_2_), channel_id=1, source_target_pairs={{3,2},{0,1},{6,5},{11,10},{8,9},{14,13},{19,18},{16,17},{22,21},{2... | collective-permute-start | bytes 1044488 | tf_op jit(solution)/shard_map/ppermute | solution.py:316
  6.3 4.7 %shard_map.65 = (bf16[1280,3072]{1,0:T(8,128)(2,1)S(1)}, bf16[128,1024]{1,0:T(8,128)(2,1)S(1)}, bf16[1024,128]{1,0:T(8,128)(2,1)S(1)}, bf16[1024,256]{1,0:T(8,12...) custom-call(bf16[136,1280]{1,0:T(8,128)(2,1)S(1)} %shard_map.64.block.refs_1_.refs_4_.refs_0_.refs_, ...), custom_call_target="tpu_custom_call" | custom-call | flops 1006632960 | bytes 3355443 | tf_op jit(solution)/shard_map/pallas_call | solution.py:33
  11.0 0.0 collective-permute-done.refs_0_.refs_5_.refs_3_
  11.0 0.0 collective-permute-done.1.refs_0_.refs_6_.refs_4_
  11.1 0.0 copy-start
  11.1 0.8 %collective-permute-start.2 = (bf16[1120,128]{1,0:T(8,128)(2,1)S(1)}, bf16[1120,128]{1,0:T(8,128)(2,1)S(1)}, u32[]{:S(2)}, u32[]{:S(2)}) collective-permute-start(bf16[1120,128]{1,0:T(8,128)(2,1)S(1)} %get-tuple-element.41), channel_id=1, source_target_pairs={{5,7},{13,15},{21,23},{29,31}} | collective-permute-start | bytes 860168 | tf_op jit(solution)/shard_map/ppermute | solution.py:316
  11.9 0.3 %collective-permute-done.3.refs_0_ = bf16[136,1280]{1,0:T(8,128)(2,1)S(1)} collective-permute-done((bf16[136,1280]{1,0:T(8,128)(2,1)S(1)}, bf16[136,1280]{1,0:T(8,128)(2,1)S(1)}, u32[]{:S(2)}, u32[]{:S(2)}) %collective-permute-start.3) | collective-permute-done | bytes 348192 | tf_op jit(solution)/shard_map/ppermute | solution.py:316
  12.3 0.8 %shard_map.68 = (f32[8,256]{1,0:T(8,128)S(1)}, f32[8,256]{1,0:T(8,128)S(1)}, f32[1024,128]{1,0:T(8,128)S(1)}, bf16[128,1024]{1,0:T(8,128)(2,1)}, bf16[1024,128]{...) custom-call(bf16[136,1280]{1,0:T(8,128)(2,1)S(1)} %collective-permute-don, ...), custom_call_target="tpu_custom_call", output_to_operand_aliasing={{0}: (13, {}), {1}: (14, {}), {2}: (15, {})} | custom-call | flops 671088640 | bytes 2236962 | tf_op jit(solution)/shard_map/pallas_call | solution.py:33
  13.0 1.3 %collective-permute-start.4 = (bf16[1120,128]{1,0:T(8,128)(2,1)S(1)}, bf16[1120,128]{1,0:T(8,128)(2,1)S(1)}, u32[]{:S(2)}, u32[]{:S(2)}) collective-permute-start(bf16[1120,128]{1,0:T(8,128)(2,1)S(1)} %get-tuple-element.45), channel_id=1, source_target_pairs={{2,3},{5,6},{10,11},{13,14},{18,19},{21,22},{26,27},{29,30}} | collective-permute-start | bytes 860168 | tf_op jit(solution)/shard_map/ppermute | solution.py:316
  14.3 0.0 collective-permute-done.2.refs_11_
  14.3 11.6 %collective-permute-done.4.refs_12_ = bf16[1120,128]{1,0:T(8,128)(2,1)S(1)} collective-permute-done((bf16[1120,128]{1,0:T(8,128)(2,1)S(1)}, bf16[1120,128]{1,0:T(8,128)(2,1)S(1)}, u32[]{:S(2)}, u32[]{:S(2)}) %collective-permute-start.4) | collective-permute-done | bytes 286752 | tf_op jit(solution)/shard_map/ppermute | solution.py:316
  25.9 0.0 copy-done
  25.9 1.4 %shard_map.69 = bf16[128,1280]{1,0:T(8,128)(2,1)} custom-call(bf16[136,1280]{1,0:T(8,128)(2,1)S(1)} %shard_map.64.block.refs_1_.refs_4_.refs_0_.refs_2_, bf16[1024,256]{1,0:T(8,128)(2,1)S(1)} %get-tuple-element.27.refs_3_.refs_1_, bf16[136,1280]{1,0:T(8,128)(2,1)S(1)} %shard_map.64.block.refs_1_.refs_4_.refs_0_.refs_2_, ...), custom_call_target="tpu_custom_call" | custom-call | flops 671088640 | bytes 2236962 | tf_op jit(solution)/shard_map/pallas_call | solution.py:33
  (2 shorter events, 0.1 us)
Async XLA Ops:
  1.3 9.7 %collective-permute-start = (bf16[136,1280]{1,0:T(8,128)(2,1)S(1)}, bf16[136,1280]{1,0:T(8,128)(2,1)S(1)}, u32[]{:S(2)}, u32[]{:S(2)}) collective-permute-start(bf16[136,1280]{1,0:T(8,128)(2,1)S(1)} %shard_map.64.block.refs_1_.refs_4_.refs_0_.refs_2_), channel_id=1, source_target_pairs={{1,2},{4,5},{9,10},{12,13},{17,18},{20,21},{25,26},{28,29}} | collective-permute-start | bytes 1044488 | tf_op jit(solution)/shard_map/ppermute | solution.py:316
  2.0 9.1 %collective-permute-start.1 = (bf16[136,1280]{1,0:T(8,128)(2,1)S(1)}, bf16[136,1280]{1,0:T(8,128)(2,1)S(1)}, u32[]{:S(2)}, u32[]{:S(2)}) collective-permute-start(bf16[136,1280]{1,0:T(8,128)(2,1)S(1)} %shard_map.64.block.refs_1_.refs_4_.refs_0_.refs_2_), channel_id=1, source_target_pairs={{0,2},{7,5},{6,7},{8,10},{15,13},{14,15},{16,18},{23,21},{22,23},{... | collective-permute-start | bytes 1044488 | tf_op jit(solution)/shard_map/ppermute | solution.py:316
  2.7 9.6 %collective-permute-start.3 = (bf16[136,1280]{1,0:T(8,128)(2,1)S(1)}, bf16[136,1280]{1,0:T(8,128)(2,1)S(1)}, u32[]{:S(2)}, u32[]{:S(2)}) collective-permute-start(bf16[136,1280]{1,0:T(8,128)(2,1)S(1)} %shard_map.64.block.refs_1_.refs_4_.refs_0_.refs_2_), channel_id=1, source_target_pairs={{3,2},{0,1},{6,5},{11,10},{8,9},{14,13},{19,18},{16,17},{22,21},{2... | collective-permute-start | bytes 1044488 | tf_op jit(solution)/shard_map/ppermute | solution.py:316
  11.1 14.9 %copy-start = (bf16[1024,1280]{1,0:T(8,128)(2,1)S(1)}, bf16[1024,1280]{1,0:T(8,128)(2,1)}, u32[]{:S(2)}) copy-start(bf16[1024,1280]{1,0:T(8,128)(2,1)} %refs_16_.1) | copy-start | bytes 7864324
  11.1 3.2 %collective-permute-start.2 = (bf16[1120,128]{1,0:T(8,128)(2,1)S(1)}, bf16[1120,128]{1,0:T(8,128)(2,1)S(1)}, u32[]{:S(2)}, u32[]{:S(2)}) collective-permute-start(bf16[1120,128]{1,0:T(8,128)(2,1)S(1)} %get-tuple-element.41), channel_id=1, source_target_pairs={{5,7},{13,15},{21,23},{29,31}} | collective-permute-start | bytes 860168 | tf_op jit(solution)/shard_map/ppermute | solution.py:316
  13.0 12.9 %collective-permute-start.4 = (bf16[1120,128]{1,0:T(8,128)(2,1)S(1)}, bf16[1120,128]{1,0:T(8,128)(2,1)S(1)}, u32[]{:S(2)}, u32[]{:S(2)}) collective-permute-start(bf16[1120,128]{1,0:T(8,128)(2,1)S(1)} %get-tuple-element.45), channel_id=1, source_target_pairs={{2,3},{5,6},{10,11},{13,14},{18,19},{21,22},{26,27},{29,30}} | collective-permute-start | bytes 860168 | tf_op jit(solution)/shard_map/ppermute | solution.py:316

commit v5 on v3

--- a/solution.py
+++ b/solution.py
@@ -12,6 +12,7 @@
 PAIR = 2
 LINES = HEADS // PAIR
 TILE = 8
+SPLIT = 2
 MASKED = -1e30
 VMEM = pltpu.VMEM
 HBM = pltpu.HBM
@@ -41,28 +42,11 @@
     )(*args)
 
 
-def plans(size):
-    result = []
-    for pivot in (size // 2, size // 2 - 1):
-        shifts = max(pivot, size - 2 - pivot)
-        slots = [("fold", t) for t in range(shifts, 0, -1)]
-        slots += [("serve", t) for t in range(1, size - pivot)]
-        result.append((pivot, slots))
-    return result
-
-
-def slot_pairs(size, pivot, slot):
-    kind, t = slot
-    if kind == "serve":
-        return [(pivot + t, pivot)]
-    return [(i, i + t) for i in range(size - t) if i + t <= pivot or i > pivot]
-
-
-def receives(size, pivot, slot, place):
-    kind, t = slot
-    if kind == "serve":
-        return place == pivot
-    return ((place >= t) & (place <= pivot)) | (place > pivot + t)
+def order_of(size, pivot, early):
+    keys, queries = list(range(pivot - 1, -1, -1)), list(range(pivot + 1, size))
+    if early and keys and queries:
+        return keys[:-1] + queries[:1] + keys[-1:] + queries[1:]
+    return keys + queries
 
 
 def embed_body(states, kinds, episode, table, out, s_in, k_in, e_in, t_in, sems):
@@ -145,19 +129,24 @@
         wide_q[place, :] = jnp.concatenate(parts, axis=1)
 
 
-def own_body(factor, block, w_qkv, w, keys, values_t, wide_q, top, total, acc, sems):
+def own_body(factor, block, w_qkv, again, w, keys, values_t, wide_q, top, total, acc, sems):
     inner = w_qkv.shape[1] // 3
+    depth = w_qkv.shape[0] // SPLIT
     copies = []
     for k in range(3):
-        part = (slice(None), slice(k * inner, (k + 1) * inner))
-        copies.append(pltpu.make_async_copy(w_qkv.at[part], w.at[part], sems.at[k]))
-        copies[k].start()
+        for r in range(SPLIT):
+            part = (slice(r * depth, (r + 1) * depth), slice(k * inner, (k + 1) * inner))
+            sem = sems.at[k * SPLIT + r]
+            copies.append(pltpu.make_async_copy(w_qkv.at[part], w.at[part], sem))
+            copies[-1].start()
+    again[...] = block[...]
     x = inputs_of(block)
     rows = x.shape[0]
-    copies[0].wait()
+    for copy in copies[:SPLIT]:
+        copy.wait()
     put_queries(x, w, wide_q)
-    copies[1].wait()
-    copies[2].wait()
+    for copy in copies[SPLIT:]:
+        copy.wait()
     put_keys_values(x, w, keys, values_t)
     place_k = lax.broadcasted_iota(jnp.int32, (rows, rows), 0)
     place_q = lax.broadcasted_iota(jnp.int32, (rows, rows), 1)
@@ -218,42 +207,86 @@
         )
 
 
-def slot_body(size, jobs, kept_at, count, factor, folds, serves, *refs):
+def slot_body(jobs, count, factor, *refs):
     refs = list(refs)
     take = lambda count: [refs.pop(0) for _ in range(count)]
-    block, mine, w, wide_q = take(4)
+    block, w = take(2)
     blocks, kept = take(count), take(2 * count)
-    take(3)
-    top, total, acc = take(3)
-    keys, values_t = take(2) if folds else (None, None)
-    packed = take(1)[0] if serves else None
+    opened = take(5) if any(job["resume"] for job in jobs) else None
+    keys, values_t = take(2)
+    packed, *state = take(5)
     place = lax.axis_index("seq")
     parity = lax.rem(lax.axis_index("dp"), 2)
-    for number, (pivot, slot) in enumerate(jobs):
-        if slot is None:
+    for number, job in enumerate(jobs):
+        if job["source"] is None:
             continue
 
-        @pl.when((parity == number) & receives(size, pivot, slot, place))
-        def _(kind=slot[0], numbers=kept_at[number]):
-            x = inputs_of(block)
-            if kind == "fold":
-                put_keys_values(x, w, keys, values_t)
-                mask = same_episode(block, mine)
-                fold(False, mask, keys, values_t, wide_q, top, total, acc, factor)
+        @pl.when((parity == number) & (place == job["pivot"]))
+        def _(job=job):
+            if job["source"] < job["pivot"]:
+                put_keys_values(inputs_of(block), w, keys, values_t)
+                if job["resume"]:
+                    queries, other_q, *before = opened
+                    for target, value in zip(state[1:], before):
+                        target[...] = value[...]
+                    mask = same_episode(block, queries)
+                    fold(False, mask, keys, values_t, other_q, *state[1:], factor)
+                    pack(*state[1:], packed)
             else:
-                other_q, *state = refs
-                put_queries(x, w, other_q)
-                for order, k in enumerate(numbers):
+                put_queries(inputs_of(block), w, state[0])
+                for order, k in enumerate(job["kept"]):
                     mask = same_episode(blocks[k], block)
                     pair = kept[2 * k : 2 * k + 2]
-                    fold(order == 0, mask, *pair, other_q, *state, factor)
-                pack(*state, packed)
+                    fold(order == 0, mask, *pair, *state, factor)
+                if not job["open"]:
+                    pack(*state[1:], packed)
+
+
+def arranged(keeps, sends, opens, jobs, count, factor, *refs):
+    resumed = any(job["resume"] for job in jobs)
+    start = 2 + 3 * count + (5 if resumed else 0)
+    before, after = refs[:start], list(refs[start:])
+    sizes, flags = (2, 1, 4), (keeps, sends, opens)
+    outs = [[after.pop(0) for _ in range(n)] if flag else None for n, flag in zip(sizes, flags)]
+    rest = [o or [after.pop(0) for _ in range(n)] for n, o in zip(sizes, outs)]
+    slot_body(jobs, count, factor, *before, *rest[0], *rest[1], *rest[2])
+
+
+def side_body(size, reach, pivots, factor, *refs):
+    block, mine, w, wide_q = refs[:4]
+    top, total, acc, keys, values_t = refs[7:]
+    place = lax.axis_index("seq")
+    parity = lax.rem(lax.axis_index("dp"), 2)
+    for number, pivot in enumerate(pivots):
+        inside = ((place >= reach) & (place < pivot)) | (place > pivot + reach)
+
+        @pl.when((parity == number) & inside)
+        def _():
+            put_keys_values(inputs_of(block), w, keys, values_t)
+            mask = same_episode(block, mine)
+            fold(False, mask, keys, values_t, wide_q, top, total, acc, factor)
+
+
+def pivot_body(pivots, kept_at, count, factor, *refs):
+    refs = list(refs)
+    take = lambda count: [refs.pop(0) for _ in range(count)]
+    mine, wide_q = take(2)
+    blocks, kept = take(count), take(2 * count)
+    state = refs[3:]
+    place = lax.axis_index("seq")
+    parity = lax.rem(lax.axis_index("dp"), 2)
+    for number, pivot in enumerate(pivots):
+
+        @pl.when((parity == number) & (place == pivot))
+        def _(numbers=kept_at[number]):
+            for k in numbers[1:]:
+                mask = same_episode(blocks[k], mine)
+                fold(False, mask, *kept[2 * k : 2 * k + 2], wide_q, *state, factor)
 
 
 def last_body(targets, factor, *refs):
-    count = len(targets)
-    packed = refs[:count]
-    top_in, total_in, acc_in, w_out, out, top, total, acc = refs[count:]
+    packed = refs[: len(targets)]
+    top_in, total_in, acc_in, w_out, out, top, total, acc = refs[len(targets) :]
     place = lax.axis_index("seq")
     parity = lax.rem(lax.axis_index("dp"), 2)
     top[...] = top_in[...]
@@ -283,8 +316,8 @@
     inner = w_out.shape[0]
     head = inner // HEADS
     factor = math.log2(math.e) / math.sqrt(head)
-    kinds = plans(size)
-    slots = max(len(s) for _, s in kinds)
+    pivots = (size // 2, size // 2 - 1)
+    orders = [order_of(size, pivot, number == 0) for number, pivot in enumerate(pivots)]
 
     def move(value, pairs_by_parity):
         pairs = []
@@ -302,10 +335,9 @@
         [VMEM(a.shape, a.dtype) for a in args] + [pltpu.SemaphoreType.DMA((len(args),))],
         spaces=[HBM] * len(args),
     )
-    jobs = [[(p, s[k] if k < len(s) else None) for p, s in kinds] for k in range(slots)]
-    moving = []
-    for job in jobs:
-        moving.append(move(mine, [slot_pairs(size, p, s) if s else [] for p, s in job]))
+    moving = [
+        move(mine, [[(o[k], p)] for o, p in zip(orders, pivots)]) for k in range(size - 1)
+    ]
 
     state = [
         shape((LINES, PAIR * rows), F32),
@@ -314,47 +346,94 @@
     ]
     wide = shape((inner, PAIR * rows), BF16)
     pair = [shape((rows, inner), BF16), shape((inner, rows), BF16)]
-    w, keys, values_t, wide_q, *now = call(
+    again, w, keys, values_t, wide_q, *now = call(
         functools.partial(own_body, factor),
-        [shape(w_qkv.shape, w_qkv.dtype)] + pair + [wide] + state,
+        [shape(mine.shape, BF16), shape(w_qkv.shape, w_qkv.dtype)] + pair + [wide] + state,
         (mine, w_qkv),
         3 * unit,
-        [pltpu.SemaphoreType.DMA((3,))],
+        [pltpu.SemaphoreType.DMA((3 * SPLIT,))],
         spaces=[VMEM, HBM],
     )
     blocks, kept, kept_at = [mine], [keys, values_t], [[0], [0]]
-    returned, targets = [], []
-    for job, block in zip(jobs, moving):
-        folds = any(s and s[0] == "fold" for _, s in job)
-        serves = any(s and s[0] == "serve" for _, s in job)
-        args = (block, mine, w, wide_q, *blocks, *kept, *now)
-        outs = state + (pair if folds else [])
-        outs += [shape((inner + 6 * HEADS, rows), BF16)] if serves else []
-        got = call(
-            functools.partial(
-                slot_body, size, job, [list(k) for k in kept_at], len(blocks), factor, folds, serves
-            ),
-            outs,
+    returned, targets, opened = [], [], None
+    for k, block in enumerate(moving):
+        jobs = []
+        for number, (pivot, order) in enumerate(zip(pivots, orders)):
+            source = order[k]
+            keep = source < pivot
+            later_keys = any(one < pivot for one in order[k + 1 :])
+            resume = keep and k > 0 and order[k - 1] > pivot
+            jobs.append(
+                dict(
+                    pivot=pivot,
+                    source=source,
+                    keep=keep,
+                    open=not keep and later_keys,
+                    resume=resume,
+                    returns=order[k - 1] if resume else source if not keep else None,
+                    kept=list(kept_at[number]),
+                )
+            )
+            if jobs[-1]["open"]:
+                jobs[-1]["returns"] = None
+        keeps = any(job["keep"] for job in jobs)
+        later = any(one < p for o, p in zip(orders, pivots) for one in o[k:]) and keeps
+        serves = [job["returns"] for job in jobs]
+        args = (block, w, *blocks, *kept)
+        if any(job["resume"] for job in jobs):
+            args = (*args, *opened)
+        inside = pair
+        result = [shape((inner + 6 * HEADS, rows), BF16), wide] + state
+        opens = any(job["open"] for job in jobs)
+        sends = any(s is not None for s in serves)
+        outs = (inside if later else []) + (result[:1] if sends else []) + (result[1:] if opens else [])
+        scratch = ([] if later else inside) + ([] if sends else result[:1]) + ([] if opens else result[1:])
+        got = list(
+            call(
+                functools.partial(arranged, later, sends, opens, jobs, len(blocks), factor),
+                outs,
+                args,
+                2 * unit,
+                [VMEM(s.shape, s.dtype) for s in scratch],
+            )
+        )
+        made = [got.pop(0) for _ in range(2)] if later else None
+        if sends:
+            back = [[] if s is None else [(p, s)] for p, s in zip(pivots, serves)]
+            returned.append(move(got.pop(0), back))
+            targets.append(serves)
+        if opens:
+            opened = [block, *got]
+        if later:
+            for number, job in enumerate(jobs):
+                if job["keep"]:
+                    kept_at[number].append(len(blocks))
+            blocks, kept = blocks + [block], kept + made
+    for reach in range(1, max(max(p, size - 1 - p) for p in pivots)):
+        pairs = [
+            [(i, i + reach) for i in range(size - reach) if i + reach < p or i > p] for p in pivots
+        ]
+        args = (move(again, pairs), mine, w, wide_q, *now)
+        now = call(
+            functools.partial(side_body, size, reach, pivots, factor),
+            state,
             args,
             2 * unit,
-            [VMEM(s.shape, s.dtype) for s in [wide] + state],
-            {len(args) - 3 + k: k for k in range(3)},
+            [VMEM(s.shape, s.dtype) for s in pair],
+            {4 + k: k for k in range(3)},
         )
-        now = got[:3]
-        if serves:
-            chosen = [(p, s[1]) if s and s[0] == "serve" else None for p, s in job]
-            returned.append(move(got[-1], [[(c[0], sum(c))] if c else [] for c in chosen]))
-            targets.append([sum(c) if c else None for c in chosen])
-        if folds:
-            for number, (pivot, slot) in enumerate(job):
-                if slot and slot[0] == "fold" and slot[1] <= pivot:
-                    kept_at[number].append(len(blocks))
-            blocks, kept = blocks + [block], kept + list(got[3:5])
-    args = (*returned, *now, w_out)
+    args = (mine, wide_q, *blocks, *kept, *now)
+    now = call(
+        functools.partial(pivot_body, pivots, kept_at, len(blocks), factor),
+        state,
+        args,
+        unit,
+        aliases={len(args) - 3 + k: k for k in range(3)},
+    )
     return call(
         functools.partial(last_body, targets, factor),
         shape((rows, w_out.shape[1]), BF16),
-        args,
+        (*returned, *now, w_out),
         2 * unit,
         [VMEM(s.shape, s.dtype) for s in state],
     )

time: 30.4 us -> 28.3 us (0.931)
  waiting for transfers between devices: 15.5 us -> 12.9 us
    ppermute x5 -> x6, waiting for transfers between devices: 15.5 us -> 12.9 us  [move(): return lax.ppermute(value, ('dp', 'seq'), pairs)]
    ppermute x5 -> x6, starting transfers between devices: 7.05 us -> 7.26 us  [move(): return lax.ppermute(value, ('dp', 'seq'), pairs)]
    pallas_call x6 -> x8, Pallas kernels: 7.48 us -> 7.68 us  [call(): pl.pallas_call(body, out_shape=outs, in_specs=[pl.BlockSpec(memory_space=...]
  transfers between devices with their start and end apart: 5 -> 6, of which waited for: 2 -> 2; matrix products, arithmetic and copies ran while one was open for 0% -> 0% of each run, Pallas kernels for 16% -> 18%
where the time goes in v5:
time: 28.3 us; the launch traced here: 27.9 us
  waiting for transfers between devices  12.9 us (46%)
  Pallas kernels  7.68 us (27%)
  starting transfers between devices  7.26 us (26%)
    ppermute x6, waiting for transfers between devices, move(): return lax.ppermute(value, ('dp', 'seq'), pairs)  12.9 us
    pallas_call x8, Pallas kernels, call(): pl.pallas_call(body, out_shape=outs, in_specs=[pl.BlockSpec(memory_space=...  7.68 us
    ppermute x6, starting transfers between devices, move(): return lax.ppermute(value, ('dp', 'seq'), pairs)  7.26 us
  transfers between devices with their start and end apart: 6, of which 2 were waited for; matrix products, arithmetic and copies ran while one was open for 0% of the time, Pallas kernels for 18%

profile of v5, /device:TPU:30, one launch (start us, length us, event | category | flops | bytes accessed | tf_op | source)
XLA Modules:
  0.0 27.9 jit_solution(3779230205418600553)
XLA Ops:
  0.0 1.3 %shard_map.64.block.refs_2_.refs_1_.refs_0_ = bf16[136,1280]{1,0:T(8,128)(2,1)S(1)} custom-call(bf16[128,1280]{1,0:T(8,128)(2,1)} %states.1, s32[1,128]{1,0:T(1,128)} %bitcast.2, s32[1,128]{1,0:T(1,128)} %bitcast.3, bf16[4,1280]{1,0:T(4,128)(2,1)} %table.1), custom_call_target="tpu_custom_call" | custom-call | flops 335544320 | bytes 1118481 | tf_op jit(solution)/shard_map/pallas_call | solution.py:33
  1.3 0.7 %collective-permute-start.1 = (bf16[136,1280]{1,0:T(8,128)(2,1)S(1)}, bf16[136,1280]{1,0:T(8,128)(2,1)S(1)}, u32[]{:S(2)}, u32[]{:S(2)}) collective-permute-start(bf16[136,1280]{1,0:T(8,128)(2,1)S(1)} %shard_map.64.block.refs_2_.refs_1_.refs_0_), channel_id=1, source_target_pairs={{1,2},{4,5},{9,10},{12,13},{17,18},{20,21},{25,26},{28,29}} | collective-permute-start | bytes 1044488 | tf_op jit(solution)/shard_map/ppermute | solution.py:326
  2.0 3.0 %collective-permute-start = (bf16[136,1280]{1,0:T(8,128)(2,1)S(1)}, bf16[136,1280]{1,0:T(8,128)(2,1)S(1)}, u32[]{:S(2)}, u32[]{:S(2)}) collective-permute-start(bf16[136,1280]{1,0:T(8,128)(2,1)S(1)} %shard_map.64.block.refs_2_.refs_1_.refs_0_), channel_id=1, source_target_pairs={{3,2},{6,5},{11,10},{14,13},{19,18},{22,21},{27,26},{30,29}} | collective-permute-start | bytes 1044488 | tf_op jit(solution)/shard_map/ppermute | solution.py:326
  5.0 0.7 %collective-permute-start.3 = (bf16[136,1280]{1,0:T(8,128)(2,1)S(1)}, bf16[136,1280]{1,0:T(8,128)(2,1)S(1)}, u32[]{:S(2)}, u32[]{:S(2)}) collective-permute-start(bf16[136,1280]{1,0:T(8,128)(2,1)S(1)} %shard_map.64.block.refs_2_.refs_1_.refs_0_), channel_id=1, source_target_pairs={{0,2},{7,5},{8,10},{15,13},{16,18},{23,21},{24,26},{31,29}} | collective-permute-start | bytes 1044488 | tf_op jit(solution)/shard_map/ppermute | solution.py:326
  5.7 4.7 %shard_map.65 = (bf16[136,1280]{1,0:T(8,128)(2,1)S(1)}, bf16[1280,3072]{1,0:T(8,128)(2,1)S(1)}, bf16[128,1024]{1,0:T(8,128)(2,1)S(1)}, bf16[1024,128]{1,0:T(8,12...) custom-call(bf16[136,1280]{1,0:T(8,128)(2,1)S(1)} %shard_map.64.bloc, ...), custom_call_target="tpu_custom_call" | custom-call | flops 1006632960 | bytes 3355443 | tf_op jit(solution)/shard_map/pallas_call | solution.py:33
  10.4 0.7 %collective-permute-start.5 = (bf16[136,1280]{1,0:T(8,128)(2,1)S(1)}, bf16[136,1280]{1,0:T(8,128)(2,1)S(1)}, u32[]{:S(2)}, u32[]{:S(2)}) collective-permute-start(bf16[136,1280]{1,0:T(8,128)(2,1)S(1)} %get-tuple-element.43), channel_id=1, source_target_pairs={{0,1},{6,7},{8,9},{14,15},{16,17},{22,23},{24,25},{30,31}} | collective-permute-start | bytes 1044488 | tf_op jit(solution)/shard_map/ppermute | solution.py:326
  11.1 0.0 collective-permute-done.1.refs_0_.refs_3_
  11.1 2.3 %collective-permute-done.refs_0_.refs_8_ = bf16[136,1280]{1,0:T(8,128)(2,1)S(1)} collective-permute-done((bf16[136,1280]{1,0:T(8,128)(2,1)S(1)}, bf16[136,1280]{1,0:T(8,128)(2,1)S(1)}, u32[]{:S(2)}, u32[]{:S(2)}) %collective-permute-start) | collective-permute-done | bytes 348192 | tf_op jit(solution)/shard_map/ppermute | solution.py:326
  13.4 0.0 collective-permute-done.3.refs_0_.refs_4_
  13.4 0.0 copy-start
  13.4 1.5 %collective-permute-start.4 = (bf16[1120,128]{1,0:T(8,128)(2,1)S(1)}, bf16[1120,128]{1,0:T(8,128)(2,1)S(1)}, u32[]{:S(2)}, u32[]{:S(2)}) collective-permute-start(bf16[1120,128]{1,0:T(8,128)(2,1)S(1)} %get-tuple-element.39), channel_id=1, source_target_pairs={{2,3},{5,7},{10,11},{13,15},{18,19},{21,23},{26,27},{29,31}} | collective-permute-start | bytes 860168 | tf_op jit(solution)/shard_map/ppermute | solution.py:326
  15.0 0.7 %collective-permute-start.2 = (bf16[1120,128]{1,0:T(8,128)(2,1)S(1)}, bf16[1120,128]{1,0:T(8,128)(2,1)S(1)}, u32[]{:S(2)}, u32[]{:S(2)}) collective-permute-start(bf16[1120,128]{1,0:T(8,128)(2,1)S(1)} %get-tuple-element.34), channel_id=1, source_target_pairs={{5,6},{13,14},{21,22},{29,30}} | collective-permute-start | bytes 860168 | tf_op jit(solution)/shard_map/ppermute | solution.py:326
  15.7 0.0 collective-permute-done.5.refs_0_
  15.7 0.2 shard_map.69
  15.9 10.5 %collective-permute-done.4.refs_1_ = bf16[1120,128]{1,0:T(8,128)(2,1)S(1)} collective-permute-done((bf16[1120,128]{1,0:T(8,128)(2,1)S(1)}, bf16[1120,128]{1,0:T(8,128)(2,1)S(1)}, u32[]{:S(2)}, u32[]{:S(2)}) %collective-permute-start.4) | collective-permute-done | bytes 286752 | tf_op jit(solution)/shard_map/ppermute | solution.py:326
  26.5 0.0 collective-permute-done.2.refs_0_
  26.5 0.0 copy-done
  26.5 1.4 %shard_map.71 = bf16[128,1280]{1,0:T(8,128)(2,1)} custom-call(bf16[1120,128]{1,0:T(8,128)(2,1)S(1)} %collective-permute-done.2.refs_0_, bf16[1120,128]{1,0:T(8,128)(2,1)S(1)} %collective-permute-done.4.refs_1_, f32[8,256]{1,0:T(8,128)S(1)} %get-tuple-element.50.refs_2_, f32[8,256]{1,0:T(8,128)S(1)} %get-tuple-element.51.refs_3_, ...), custom_call_target="tpu_custom_call" | custom-call | flops 671088640 | bytes 2236962 | tf_op jit(solution)/shard_map/pallas_call | solution.py:33
  (4 shorter events, 0.1 us)
Async XLA Ops:
  1.3 9.8 %collective-permute-start.1 = (bf16[136,1280]{1,0:T(8,128)(2,1)S(1)}, bf16[136,1280]{1,0:T(8,128)(2,1)S(1)}, u32[]{:S(2)}, u32[]{:S(2)}) collective-permute-start(bf16[136,1280]{1,0:T(8,128)(2,1)S(1)} %shard_map.64.block.refs_2_.refs_1_.refs_0_), channel_id=1, source_target_pairs={{1,2},{4,5},{9,10},{12,13},{17,18},{20,21},{25,26},{28,29}} | collective-permute-start | bytes 1044488 | tf_op jit(solution)/shard_map/ppermute | solution.py:326
  2.0 11.4 %collective-permute-start = (bf16[136,1280]{1,0:T(8,128)(2,1)S(1)}, bf16[136,1280]{1,0:T(8,128)(2,1)S(1)}, u32[]{:S(2)}, u32[]{:S(2)}) collective-permute-start(bf16[136,1280]{1,0:T(8,128)(2,1)S(1)} %shard_map.64.block.refs_2_.refs_1_.refs_0_), channel_id=1, source_target_pairs={{3,2},{6,5},{11,10},{14,13},{19,18},{22,21},{27,26},{30,29}} | collective-permute-start | bytes 1044488 | tf_op jit(solution)/shard_map/ppermute | solution.py:326
  5.0 8.5 %collective-permute-start.3 = (bf16[136,1280]{1,0:T(8,128)(2,1)S(1)}, bf16[136,1280]{1,0:T(8,128)(2,1)S(1)}, u32[]{:S(2)}, u32[]{:S(2)}) collective-permute-start(bf16[136,1280]{1,0:T(8,128)(2,1)S(1)} %shard_map.64.block.refs_2_.refs_1_.refs_0_), channel_id=1, source_target_pairs={{0,2},{7,5},{8,10},{15,13},{16,18},{23,21},{24,26},{31,29}} | collective-permute-start | bytes 1044488 | tf_op jit(solution)/shard_map/ppermute | solution.py:326
  10.4 5.3 %collective-permute-start.5 = (bf16[136,1280]{1,0:T(8,128)(2,1)S(1)}, bf16[136,1280]{1,0:T(8,128)(2,1)S(1)}, u32[]{:S(2)}, u32[]{:S(2)}) collective-permute-start(bf16[136,1280]{1,0:T(8,128)(2,1)S(1)} %get-tuple-element.43), channel_id=1, source_target_pairs={{0,1},{6,7},{8,9},{14,15},{16,17},{22,23},{24,25},{30,31}} | collective-permute-start | bytes 1044488 | tf_op jit(solution)/shard_map/ppermute | solution.py:326
  13.4 13.1 %copy-start = (bf16[1024,1280]{1,0:T(8,128)(2,1)S(1)}, bf16[1024,1280]{1,0:T(8,128)(2,1)}, u32[]{:S(2)}) copy-start(bf16[1024,1280]{1,0:T(8,128)(2,1)} %refs_5_.1) | copy-start | bytes 7864324
  13.4 13.0 %collective-permute-start.4 = (bf16[1120,128]{1,0:T(8,128)(2,1)S(1)}, bf16[1120,128]{1,0:T(8,128)(2,1)S(1)}, u32[]{:S(2)}, u32[]{:S(2)}) collective-permute-start(bf16[1120,128]{1,0:T(8,128)(2,1)S(1)} %get-tuple-element.39), channel_id=1, source_target_pairs={{2,3},{5,7},{10,11},{13,15},{18,19},{21,23},{26,27},{29,31}} | collective-permute-start | bytes 860168 | tf_op jit(solution)/shard_map/ppermute | solution.py:326
  15.0 11.5 %collective-permute-start.2 = (bf16[1120,128]{1,0:T(8,128)(2,1)S(1)}, bf16[1120,128]{1,0:T(8,128)(2,1)S(1)}, u32[]{:S(2)}, u32[]{:S(2)}) collective-permute-start(bf16[1120,128]{1,0:T(8,128)(2,1)S(1)} %get-tuple-element.34), channel_id=1, source_target_pairs={{5,6},{13,14},{21,22},{29,30}} | collective-permute-start | bytes 860168 | tf_op jit(solution)/shard_map/ppermute | solution.py:326

commit v6 on v5

--- a/solution.py
+++ b/solution.py
@@ -12,7 +12,6 @@
 PAIR = 2
 LINES = HEADS // PAIR
 TILE = 8
-SPLIT = 2
 MASKED = -1e30
 VMEM = pltpu.VMEM
 HBM = pltpu.HBM
@@ -129,24 +128,11 @@
         wide_q[place, :] = jnp.concatenate(parts, axis=1)
 
 
-def own_body(factor, block, w_qkv, again, w, keys, values_t, wide_q, top, total, acc, sems):
-    inner = w_qkv.shape[1] // 3
-    depth = w_qkv.shape[0] // SPLIT
-    copies = []
-    for k in range(3):
-        for r in range(SPLIT):
-            part = (slice(r * depth, (r + 1) * depth), slice(k * inner, (k + 1) * inner))
-            sem = sems.at[k * SPLIT + r]
-            copies.append(pltpu.make_async_copy(w_qkv.at[part], w.at[part], sem))
-            copies[-1].start()
+def own_body(factor, block, w, again, keys, values_t, wide_q, top, total, acc):
     again[...] = block[...]
     x = inputs_of(block)
     rows = x.shape[0]
-    for copy in copies[:SPLIT]:
-        copy.wait()
     put_queries(x, w, wide_q)
-    for copy in copies[SPLIT:]:
-        copy.wait()
     put_keys_values(x, w, keys, values_t)
     place_k = lax.broadcasted_iota(jnp.int32, (rows, rows), 0)
     place_q = lax.broadcasted_iota(jnp.int32, (rows, rows), 1)
@@ -331,7 +317,7 @@
         embed_body,
         shape((rows + TILE, width), BF16),
         args,
-        unit,
+        30 * unit,
         [VMEM(a.shape, a.dtype) for a in args] + [pltpu.SemaphoreType.DMA((len(args),))],
         spaces=[HBM] * len(args),
     )
@@ -346,13 +332,11 @@
     ]
     wide = shape((inner, PAIR * rows), BF16)
     pair = [shape((rows, inner), BF16), shape((inner, rows), BF16)]
-    again, w, keys, values_t, wide_q, *now = call(
+    again, keys, values_t, wide_q, *now = call(
         functools.partial(own_body, factor),
-        [shape(mine.shape, BF16), shape(w_qkv.shape, w_qkv.dtype)] + pair + [wide] + state,
+        [shape(mine.shape, BF16)] + pair + [wide] + state,
         (mine, w_qkv),
         3 * unit,
-        [pltpu.SemaphoreType.DMA((3 * SPLIT,))],
-        spaces=[VMEM, HBM],
     )
     blocks, kept, kept_at = [mine], [keys, values_t], [[0], [0]]
     returned, targets, opened = [], [], None
@@ -379,7 +363,7 @@
         keeps = any(job["keep"] for job in jobs)
         later = any(one < p for o, p in zip(orders, pivots) for one in o[k:]) and keeps
         serves = [job["returns"] for job in jobs]
-        args = (block, w, *blocks, *kept)
+        args = (block, w_qkv, *blocks, *kept)
         if any(job["resume"] for job in jobs):
             args = (*args, *opened)
         inside = pair
@@ -413,7 +397,7 @@
         pairs = [
             [(i, i + reach) for i in range(size - reach) if i + reach < p or i > p] for p in pivots
         ]
-        args = (move(again, pairs), mine, w, wide_q, *now)
+        args = (move(again, pairs), mine, w_qkv, wide_q, *now)
         now = call(
             functools.partial(side_body, size, reach, pivots, factor),
             state,

time: 28.3 us -> 28.6 us (1.011)
  waiting for transfers between devices: 12.9 us -> 16 us
  Pallas kernels: 7.68 us -> 4.67 us
    ppermute x6, waiting for transfers between devices: 12.9 us -> 16 us  [move(): return lax.ppermute(value, ('dp', 'seq'), pairs)]
    pallas_call x8, Pallas kernels: 7.68 us -> 4.67 us  [call(): pl.pallas_call(body, out_shape=outs, in_specs=[pl.BlockSpec(memory_space=...]
  transfers between devices with their start and end apart: 6 -> 6, of which waited for: 2 -> 2; matrix products, arithmetic and copies ran while one was open for 0% -> 0% of each run, Pallas kernels for 18% -> 6%
where the time goes in v6:
time: 28.6 us; the launch traced here: 28.3 us
  waiting for transfers between devices  16 us (56%)
  starting transfers between devices  7.52 us (26%)
  Pallas kernels  4.67 us (16%)
    ppermute x6, waiting for transfers between devices, move(): return lax.ppermute(value, ('dp', 'seq'), pairs)  16 us
    ppermute x6, starting transfers between devices, move(): return lax.ppermute(value, ('dp', 'seq'), pairs)  7.52 us
    pallas_call x8, Pallas kernels, call(): pl.pallas_call(body, out_shape=outs, in_specs=[pl.BlockSpec(memory_space=...  4.67 us
  transfers between devices with their start and end apart: 6, of which 2 were waited for; matrix products, arithmetic and copies ran while one was open for 0% of the time, Pallas kernels for 6%

profile of v6, /device:TPU:30, one launch (start us, length us, event | category | flops | bytes accessed | tf_op | source)
XLA Modules:
  0.0 28.3 jit_solution(4838595869771085789)
XLA Ops:
  0.0 0.0 copy-start
  0.0 1.4 %shard_map.64.block.refs_2_.refs_1_.refs_0_ = bf16[136,1280]{1,0:T(8,128)(2,1)S(1)} custom-call(bf16[128,1280]{1,0:T(8,128)(2,1)} %states.1, s32[1,128]{1,0:T(1,128)} %bitcast.2, s32[1,128]{1,0:T(1,128)} %bitcast.3, bf16[4,1280]{1,0:T(4,128)(2,1)} %table.1), custom_call_target="tpu_custom_call" | custom-call | flops 10066329600 | bytes 33554432 | tf_op jit(solution)/shard_map/pallas_call | solution.py:32
  1.5 0.8 %collective-permute-start.1 = (bf16[136,1280]{1,0:T(8,128)(2,1)S(1)}, bf16[136,1280]{1,0:T(8,128)(2,1)S(1)}, u32[]{:S(2)}, u32[]{:S(2)}) collective-permute-start(bf16[136,1280]{1,0:T(8,128)(2,1)S(1)} %shard_map.64.block.refs_2_.refs_1_.refs_0_), channel_id=1, source_target_pairs={{1,2},{4,5},{9,10},{12,13},{17,18},{20,21},{25,26},{28,29}} | collective-permute-start | bytes 1044488 | tf_op jit(solution)/shard_map/ppermute | solution.py:312
  2.3 3.1 %collective-permute-start = (bf16[136,1280]{1,0:T(8,128)(2,1)S(1)}, bf16[136,1280]{1,0:T(8,128)(2,1)S(1)}, u32[]{:S(2)}, u32[]{:S(2)}) collective-permute-start(bf16[136,1280]{1,0:T(8,128)(2,1)S(1)} %shard_map.64.block.refs_2_.refs_1_.refs_0_), channel_id=1, source_target_pairs={{3,2},{6,5},{11,10},{14,13},{19,18},{22,21},{27,26},{30,29}} | collective-permute-start | bytes 1044488 | tf_op jit(solution)/shard_map/ppermute | solution.py:312
  5.4 0.7 %collective-permute-start.3 = (bf16[136,1280]{1,0:T(8,128)(2,1)S(1)}, bf16[136,1280]{1,0:T(8,128)(2,1)S(1)}, u32[]{:S(2)}, u32[]{:S(2)}) collective-permute-start(bf16[136,1280]{1,0:T(8,128)(2,1)S(1)} %shard_map.64.block.refs_2_.refs_1_.refs_0_), channel_id=1, source_target_pairs={{0,2},{7,5},{8,10},{15,13},{16,18},{23,21},{24,26},{31,29}} | collective-permute-start | bytes 1044488 | tf_op jit(solution)/shard_map/ppermute | solution.py:312
  6.1 0.0 copy-done
  6.1 1.7 %shard_map.65 = (bf16[136,1280]{1,0:T(8,128)(2,1)S(1)}, bf16[128,1024]{1,0:T(8,128)(2,1)S(1)}, bf16[1024,128]{1,0:T(8,128)(2,1)S(1)}, bf16[1024,256]{1,0:T(8,128...) custom-call(bf16[136,1280]{1,0:T(8,128)(2,1)S(1)} %shard_map.64.block.refs_2_.refs_1_.refs_0_, ...), custom_call_target="tpu_custom_call" | custom-call | flops 1006632960 | bytes 3355443 | tf_op jit(solution)/shard_map/pallas_call | solution.py:32
  7.8 0.7 %collective-permute-start.5 = (bf16[136,1280]{1,0:T(8,128)(2,1)S(1)}, bf16[136,1280]{1,0:T(8,128)(2,1)S(1)}, u32[]{:S(2)}, u32[]{:S(2)}) collective-permute-start(bf16[136,1280]{1,0:T(8,128)(2,1)S(1)} %get-tuple-element.41), channel_id=1, source_target_pairs={{0,1},{6,7},{8,9},{14,15},{16,17},{22,23},{24,25},{30,31}} | collective-permute-start | bytes 1044488 | tf_op jit(solution)/shard_map/ppermute | solution.py:312
  8.5 0.0 collective-permute-done.1.refs_0_.refs_3_
  8.5 5.3 %collective-permute-done.refs_0_.refs_8_ = bf16[136,1280]{1,0:T(8,128)(2,1)S(1)} collective-permute-done((bf16[136,1280]{1,0:T(8,128)(2,1)S(1)}, bf16[136,1280]{1,0:T(8,128)(2,1)S(1)}, u32[]{:S(2)}, u32[]{:S(2)}) %collective-permute-start) | collective-permute-done | bytes 348192 | tf_op jit(solution)/shard_map/ppermute | solution.py:312
  13.8 0.7 %collective-permute-start.2 = (bf16[1120,128]{1,0:T(8,128)(2,1)S(1)}, bf16[1120,128]{1,0:T(8,128)(2,1)S(1)}, u32[]{:S(2)}, u32[]{:S(2)}) collective-permute-start(bf16[1120,128]{1,0:T(8,128)(2,1)S(1)} %get-tuple-element.32), channel_id=1, source_target_pairs={{5,6},{13,14},{21,22},{29,30}} | collective-permute-start | bytes 860168 | tf_op jit(solution)/shard_map/ppermute | solution.py:312
  14.5 0.0 collective-permute-done.3.refs_0_.refs_4_
  14.6 0.0 copy-start.1
  14.6 1.6 %collective-permute-start.4 = (bf16[1120,128]{1,0:T(8,128)(2,1)S(1)}, bf16[1120,128]{1,0:T(8,128)(2,1)S(1)}, u32[]{:S(2)}, u32[]{:S(2)}) collective-permute-start(bf16[1120,128]{1,0:T(8,128)(2,1)S(1)} %get-tuple-element.37), channel_id=1, source_target_pairs={{2,3},{5,7},{10,11},{13,15},{18,19},{21,23},{26,27},{29,31}} | collective-permute-start | bytes 860168 | tf_op jit(solution)/shard_map/ppermute | solution.py:312
  16.1 0.0 collective-permute-done.5.refs_0_
  16.2 0.0 collective-permute-done.2.refs_0_
  16.2 10.7 %collective-permute-done.4.refs_1_ = bf16[1120,128]{1,0:T(8,128)(2,1)S(1)} collective-permute-done((bf16[1120,128]{1,0:T(8,128)(2,1)S(1)}, bf16[1120,128]{1,0:T(8,128)(2,1)S(1)}, u32[]{:S(2)}, u32[]{:S(2)}) %collective-permute-start.4) | collective-permute-done | bytes 286752 | tf_op jit(solution)/shard_map/ppermute | solution.py:312
  26.9 0.0 copy-done.1
  26.9 1.4 %shard_map.71 = bf16[128,1280]{1,0:T(8,128)(2,1)} custom-call(bf16[1120,128]{1,0:T(8,128)(2,1)S(1)} %collective-permute-done.2.refs_0_, bf16[1120,128]{1,0:T(8,128)(2,1)S(1)} %collective-permute-done.4.refs_1_, f32[8,256]{1,0:T(8,128)S(1)} %get-tuple-element.48.refs_2_, f32[8,256]{1,0:T(8,128)S(1)} %get-tuple-element.49.refs_3_, ...), custom_call_target="tpu_custom_call" | custom-call | flops 671088640 | bytes 2236962 | tf_op jit(solution)/shard_map/pallas_call | solution.py:32
  (5 shorter events, 0.1 us)
Async XLA Ops:
  0.0 6.1 %copy-start = (bf16[1280,3072]{1,0:T(8,128)(2,1)S(1)}, bf16[1280,3072]{1,0:T(8,128)(2,1)}, u32[]{:S(2)}) copy-start(bf16[1280,3072]{1,0:T(8,128)(2,1)} %refs_2_.1) | copy-start | bytes 23592964
  1.5 7.1 %collective-permute-start.1 = (bf16[136,1280]{1,0:T(8,128)(2,1)S(1)}, bf16[136,1280]{1,0:T(8,128)(2,1)S(1)}, u32[]{:S(2)}, u32[]{:S(2)}) collective-permute-start(bf16[136,1280]{1,0:T(8,128)(2,1)S(1)} %shard_map.64.block.refs_2_.refs_1_.refs_0_), channel_id=1, source_target_pairs={{1,2},{4,5},{9,10},{12,13},{17,18},{20,21},{25,26},{28,29}} | collective-permute-start | bytes 1044488 | tf_op jit(solution)/shard_map/ppermute | solution.py:312
  2.3 11.6 %collective-permute-start = (bf16[136,1280]{1,0:T(8,128)(2,1)S(1)}, bf16[136,1280]{1,0:T(8,128)(2,1)S(1)}, u32[]{:S(2)}, u32[]{:S(2)}) collective-permute-start(bf16[136,1280]{1,0:T(8,128)(2,1)S(1)} %shard_map.64.block.refs_2_.refs_1_.refs_0_), channel_id=1, source_target_pairs={{3,2},{6,5},{11,10},{14,13},{19,18},{22,21},{27,26},{30,29}} | collective-permute-start | bytes 1044488 | tf_op jit(solution)/shard_map/ppermute | solution.py:312
  5.4 9.1 %collective-permute-start.3 = (bf16[136,1280]{1,0:T(8,128)(2,1)S(1)}, bf16[136,1280]{1,0:T(8,128)(2,1)S(1)}, u32[]{:S(2)}, u32[]{:S(2)}) collective-permute-start(bf16[136,1280]{1,0:T(8,128)(2,1)S(1)} %shard_map.64.block.refs_2_.refs_1_.refs_0_), channel_id=1, source_target_pairs={{0,2},{7,5},{8,10},{15,13},{16,18},{23,21},{24,26},{31,29}} | collective-permute-start | bytes 1044488 | tf_op jit(solution)/shard_map/ppermute | solution.py:312
  7.8 8.3 %collective-permute-start.5 = (bf16[136,1280]{1,0:T(8,128)(2,1)S(1)}, bf16[136,1280]{1,0:T(8,128)(2,1)S(1)}, u32[]{:S(2)}, u32[]{:S(2)}) collective-permute-start(bf16[136,1280]{1,0:T(8,128)(2,1)S(1)} %get-tuple-element.41), channel_id=1, source_target_pairs={{0,1},{6,7},{8,9},{14,15},{16,17},{22,23},{24,25},{30,31}} | collective-permute-start | bytes 1044488 | tf_op jit(solution)/shard_map/ppermute | solution.py:312
  13.8 2.4 %collective-permute-start.2 = (bf16[1120,128]{1,0:T(8,128)(2,1)S(1)}, bf16[1120,128]{1,0:T(8,128)(2,1)S(1)}, u32[]{:S(2)}, u32[]{:S(2)}) collective-permute-start(bf16[1120,128]{1,0:T(8,128)(2,1)S(1)} %get-tuple-element.32), channel_id=1, source_target_pairs={{5,6},{13,14},{21,22},{29,30}} | collective-permute-start | bytes 860168 | tf_op jit(solution)/shard_map/ppermute | solution.py:312
  14.6 12.3 %copy-start.1 = (bf16[1024,1280]{1,0:T(8,128)(2,1)S(1)}, bf16[1024,1280]{1,0:T(8,128)(2,1)}, u32[]{:S(2)}) copy-start(bf16[1024,1280]{1,0:T(8,128)(2,1)} %refs_5_.1) | copy-start | bytes 7864324
  14.6 12.3 %collective-permute-start.4 = (bf16[1120,128]{1,0:T(8,128)(2,1)S(1)}, bf16[1120,128]{1,0:T(8,128)(2,1)S(1)}, u32[]{:S(2)}, u32[]{:S(2)}) collective-permute-start(bf16[1120,128]{1,0:T(8,128)(2,1)S(1)} %get-tuple-element.37), channel_id=1, source_target_pairs={{2,3},{5,7},{10,11},{13,15},{18,19},{21,23},{26,27},{29,31}} | collective-permute-start | bytes 860168 | tf_op jit(solution)/shard_map/ppermute | solution.py:312

commit v7 on v6

--- a/solution.py
+++ b/solution.py
@@ -41,11 +41,8 @@
     )(*args)
 
 
-def order_of(size, pivot, early):
-    keys, queries = list(range(pivot - 1, -1, -1)), list(range(pivot + 1, size))
-    if early and keys and queries:
-        return keys[:-1] + queries[:1] + keys[-1:] + queries[1:]
-    return keys + queries
+def order_of(size, pivot):
+    return list(range(pivot - 1, -1, -1)) + list(range(size - 1, pivot, -1))
 
 
 def embed_body(states, kinds, episode, table, out, s_in, k_in, e_in, t_in, sems):
@@ -303,7 +300,7 @@
     head = inner // HEADS
     factor = math.log2(math.e) / math.sqrt(head)
     pivots = (size // 2, size // 2 - 1)
-    orders = [order_of(size, pivot, number == 0) for number, pivot in enumerate(pivots)]
+    orders = [order_of(size, pivot) for pivot in pivots]
 
     def move(value, pairs_by_parity):
         pairs = []

time: 28.6 us -> 29.6 us (1.035)
  starting transfers between devices: 7.52 us -> 8.13 us
  waiting for transfers between devices: 16 us -> 16.5 us
    ppermute x6, starting transfers between devices: 7.52 us -> 8.13 us  [move(): return lax.ppermute(value, ('dp', 'seq'), pairs)]
    ppermute x6, waiting for transfers between devices: 16 us -> 16.5 us  [move(): return lax.ppermute(value, ('dp', 'seq'), pairs)]
where the time goes in v7:
time: 29.6 us; the launch traced here: 29.4 us
  waiting for transfers between devices  16.5 us (56%)
  starting transfers between devices  8.13 us (27%)
  Pallas kernels  4.67 us (16%)
    ppermute x6, waiting for transfers between devices, move(): return lax.ppermute(value, ('dp', 'seq'), pairs)  16.5 us
    ppermute x6, starting transfers between devices, move(): return lax.ppermute(value, ('dp', 'seq'), pairs)  8.13 us
    pallas_call x8, Pallas kernels, call(): pl.pallas_call(body, out_shape=outs, in_specs=[pl.BlockSpec(memory_space=...  4.67 us
  transfers between devices with their start and end apart: 6, of which 2 were waited for; matrix products, arithmetic and copies ran while one was open for 0% of the time, Pallas kernels for 6%

profile of v7, /device:TPU:30, one launch (start us, length us, event | category | flops | bytes accessed | tf_op | source)
XLA Modules:
  0.0 29.4 jit_solution(7391673159808793105)
XLA Ops:
  0.0 0.0 copy-start
  0.0 1.4 %shard_map.64.block.refs_2_.refs_1_.refs_0_ = bf16[136,1280]{1,0:T(8,128)(2,1)S(1)} custom-call(bf16[128,1280]{1,0:T(8,128)(2,1)} %states.1, s32[1,128]{1,0:T(1,128)} %bitcast.2, s32[1,128]{1,0:T(1,128)} %bitcast.3, bf16[4,1280]{1,0:T(4,128)(2,1)} %table.1), custom_call_target="tpu_custom_call" | custom-call | flops 10066329600 | bytes 33554432 | tf_op jit(solution)/shard_map/pallas_call | solution.py:32
  1.5 0.8 %collective-permute-start.1 = (bf16[136,1280]{1,0:T(8,128)(2,1)S(1)}, bf16[136,1280]{1,0:T(8,128)(2,1)S(1)}, u32[]{:S(2)}, u32[]{:S(2)}) collective-permute-start(bf16[136,1280]{1,0:T(8,128)(2,1)S(1)} %shard_map.64.block.refs_2_.refs_1_.refs_0_), channel_id=1, source_target_pairs={{1,2},{4,5},{9,10},{12,13},{17,18},{20,21},{25,26},{28,29}} | collective-permute-start | bytes 1044488 | tf_op jit(solution)/shard_map/ppermute | solution.py:309
  2.3 0.8 %collective-permute-start = (bf16[136,1280]{1,0:T(8,128)(2,1)S(1)}, bf16[136,1280]{1,0:T(8,128)(2,1)S(1)}, u32[]{:S(2)}, u32[]{:S(2)}) collective-permute-start(bf16[136,1280]{1,0:T(8,128)(2,1)S(1)} %shard_map.64.block.refs_2_.refs_1_.refs_0_), channel_id=1, source_target_pairs={{0,2},{7,5},{8,10},{15,13},{16,18},{23,21},{24,26},{31,29}} | collective-permute-start | bytes 1044488 | tf_op jit(solution)/shard_map/ppermute | solution.py:309
  3.1 3.6 %collective-permute-start.3 = (bf16[136,1280]{1,0:T(8,128)(2,1)S(1)}, bf16[136,1280]{1,0:T(8,128)(2,1)S(1)}, u32[]{:S(2)}, u32[]{:S(2)}) collective-permute-start(bf16[136,1280]{1,0:T(8,128)(2,1)S(1)} %shard_map.64.block.refs_2_.refs_1_.refs_0_), channel_id=1, source_target_pairs={{3,2},{6,5},{11,10},{14,13},{19,18},{22,21},{27,26},{30,29}} | collective-permute-start | bytes 1044488 | tf_op jit(solution)/shard_map/ppermute | solution.py:309
  6.7 0.0 copy-done
  6.7 1.7 %shard_map.65 = (bf16[136,1280]{1,0:T(8,128)(2,1)S(1)}, bf16[128,1024]{1,0:T(8,128)(2,1)S(1)}, bf16[1024,128]{1,0:T(8,128)(2,1)S(1)}, bf16[1024,256]{1,0:T(8,128...) custom-call(bf16[136,1280]{1,0:T(8,128)(2,1)S(1)} %shard_map.64.block.refs_2_.refs_1_.refs_0_, ...), custom_call_target="tpu_custom_call" | custom-call | flops 1006632960 | bytes 3355443 | tf_op jit(solution)/shard_map/pallas_call | solution.py:32
  8.4 0.7 %collective-permute-start.5 = (bf16[136,1280]{1,0:T(8,128)(2,1)S(1)}, bf16[136,1280]{1,0:T(8,128)(2,1)S(1)}, u32[]{:S(2)}, u32[]{:S(2)}) collective-permute-start(bf16[136,1280]{1,0:T(8,128)(2,1)S(1)} %get-tuple-element.31), channel_id=1, source_target_pairs={{0,1},{6,7},{8,9},{14,15},{16,17},{22,23},{24,25},{30,31}} | collective-permute-start | bytes 1044488 | tf_op jit(solution)/shard_map/ppermute | solution.py:309
  9.1 0.0 collective-permute-done.1.refs_0_.refs_3_
  9.2 0.0 collective-permute-done.refs_0_.refs_4_
  9.2 3.5 %collective-permute-done.3.refs_0_ = bf16[136,1280]{1,0:T(8,128)(2,1)S(1)} collective-permute-done((bf16[136,1280]{1,0:T(8,128)(2,1)S(1)}, bf16[136,1280]{1,0:T(8,128)(2,1)S(1)}, u32[]{:S(2)}, u32[]{:S(2)}) %collective-permute-start.3) | collective-permute-done | bytes 348192 | tf_op jit(solution)/shard_map/ppermute | solution.py:309
  12.7 0.0 copy-start.1
  12.7 1.5 %collective-permute-start.4 = (bf16[1120,128]{1,0:T(8,128)(2,1)S(1)}, bf16[1120,128]{1,0:T(8,128)(2,1)S(1)}, u32[]{:S(2)}, u32[]{:S(2)}) collective-permute-start(bf16[1120,128]{1,0:T(8,128)(2,1)S(1)} %shard_map.68), channel_id=1, source_target_pairs={{2,3},{5,6},{10,11},{13,14},{18,19},{21,22},{26,27},{29,30}} | collective-permute-start | bytes 860168 | tf_op jit(solution)/shard_map/ppermute | solution.py:309
  14.2 0.7 %collective-permute-start.2 = (bf16[1120,128]{1,0:T(8,128)(2,1)S(1)}, bf16[1120,128]{1,0:T(8,128)(2,1)S(1)}, u32[]{:S(2)}, u32[]{:S(2)}) collective-permute-start(bf16[1120,128]{1,0:T(8,128)(2,1)S(1)} %get-tuple-element.27), channel_id=1, source_target_pairs={{5,7},{13,15},{21,23},{29,31}} | collective-permute-start | bytes 860168 | tf_op jit(solution)/shard_map/ppermute | solution.py:309
  14.9 0.0 collective-permute-done.5.refs_0_
  15.0 12.9 %collective-permute-done.4.refs_1_ = bf16[1120,128]{1,0:T(8,128)(2,1)S(1)} collective-permute-done((bf16[1120,128]{1,0:T(8,128)(2,1)S(1)}, bf16[1120,128]{1,0:T(8,128)(2,1)S(1)}, u32[]{:S(2)}, u32[]{:S(2)}) %collective-permute-start.4) | collective-permute-done | bytes 286752 | tf_op jit(solution)/shard_map/ppermute | solution.py:309
  28.0 0.0 collective-permute-done.2.refs_0_
  28.0 0.0 copy-done.1
  28.0 1.4 %shard_map.71 = bf16[128,1280]{1,0:T(8,128)(2,1)} custom-call(bf16[1120,128]{1,0:T(8,128)(2,1)S(1)} %collective-permute-done.2.refs_0_, bf16[1120,128]{1,0:T(8,128)(2,1)S(1)} %collective-permute-done.4.refs_1_, f32[8,256]{1,0:T(8,128)S(1)} %get-tuple-element.38.refs_2_, f32[8,256]{1,0:T(8,128)S(1)} %get-tuple-element.39.refs_3_, ...), custom_call_target="tpu_custom_call" | custom-call | flops 671088640 | bytes 2236962 | tf_op jit(solution)/shard_map/pallas_call | solution.py:32
  (5 shorter events, 0.1 us)
Async XLA Ops:
  0.0 6.7 %copy-start = (bf16[1280,3072]{1,0:T(8,128)(2,1)S(1)}, bf16[1280,3072]{1,0:T(8,128)(2,1)}, u32[]{:S(2)}) copy-start(bf16[1280,3072]{1,0:T(8,128)(2,1)} %refs_2_.1) | copy-start | bytes 23592964
  1.5 7.7 %collective-permute-start.1 = (bf16[136,1280]{1,0:T(8,128)(2,1)S(1)}, bf16[136,1280]{1,0:T(8,128)(2,1)S(1)}, u32[]{:S(2)}, u32[]{:S(2)}) collective-permute-start(bf16[136,1280]{1,0:T(8,128)(2,1)S(1)} %shard_map.64.block.refs_2_.refs_1_.refs_0_), channel_id=1, source_target_pairs={{1,2},{4,5},{9,10},{12,13},{17,18},{20,21},{25,26},{28,29}} | collective-permute-start | bytes 1044488 | tf_op jit(solution)/shard_map/ppermute | solution.py:309
  2.3 6.9 %collective-permute-start = (bf16[136,1280]{1,0:T(8,128)(2,1)S(1)}, bf16[136,1280]{1,0:T(8,128)(2,1)S(1)}, u32[]{:S(2)}, u32[]{:S(2)}) collective-permute-start(bf16[136,1280]{1,0:T(8,128)(2,1)S(1)} %shard_map.64.block.refs_2_.refs_1_.refs_0_), channel_id=1, source_target_pairs={{0,2},{7,5},{8,10},{15,13},{16,18},{23,21},{24,26},{31,29}} | collective-permute-start | bytes 1044488 | tf_op jit(solution)/shard_map/ppermute | solution.py:309
  3.1 9.6 %collective-permute-start.3 = (bf16[136,1280]{1,0:T(8,128)(2,1)S(1)}, bf16[136,1280]{1,0:T(8,128)(2,1)S(1)}, u32[]{:S(2)}, u32[]{:S(2)}) collective-permute-start(bf16[136,1280]{1,0:T(8,128)(2,1)S(1)} %shard_map.64.block.refs_2_.refs_1_.refs_0_), channel_id=1, source_target_pairs={{3,2},{6,5},{11,10},{14,13},{19,18},{22,21},{27,26},{30,29}} | collective-permute-start | bytes 1044488 | tf_op jit(solution)/shard_map/ppermute | solution.py:309
  8.4 6.5 %collective-permute-start.5 = (bf16[136,1280]{1,0:T(8,128)(2,1)S(1)}, bf16[136,1280]{1,0:T(8,128)(2,1)S(1)}, u32[]{:S(2)}, u32[]{:S(2)}) collective-permute-start(bf16[136,1280]{1,0:T(8,128)(2,1)S(1)} %get-tuple-element.31), channel_id=1, source_target_pairs={{0,1},{6,7},{8,9},{14,15},{16,17},{22,23},{24,25},{30,31}} | collective-permute-start | bytes 1044488 | tf_op jit(solution)/shard_map/ppermute | solution.py:309
  12.7 15.3 %copy-start.1 = (bf16[1024,1280]{1,0:T(8,128)(2,1)S(1)}, bf16[1024,1280]{1,0:T(8,128)(2,1)}, u32[]{:S(2)}) copy-start(bf16[1024,1280]{1,0:T(8,128)(2,1)} %refs_5_.1) | copy-start | bytes 7864324
  12.7 15.3 %collective-permute-start.4 = (bf16[1120,128]{1,0:T(8,128)(2,1)S(1)}, bf16[1120,128]{1,0:T(8,128)(2,1)S(1)}, u32[]{:S(2)}, u32[]{:S(2)}) collective-permute-start(bf16[1120,128]{1,0:T(8,128)(2,1)S(1)} %shard_map.68), channel_id=1, source_target_pairs={{2,3},{5,6},{10,11},{13,14},{18,19},{21,22},{26,27},{29,30}} | collective-permute-start | bytes 860168 | tf_op jit(solution)/shard_map/ppermute | solution.py:309
  14.2 13.7 %collective-permute-start.2 = (bf16[1120,128]{1,0:T(8,128)(2,1)S(1)}, bf16[1120,128]{1,0:T(8,128)(2,1)S(1)}, u32[]{:S(2)}, u32[]{:S(2)}) collective-permute-start(bf16[1120,128]{1,0:T(8,128)(2,1)S(1)} %get-tuple-element.27), channel_id=1, source_target_pairs={{5,7},{13,15},{21,23},{29,31}} | collective-permute-start | bytes 860168 | tf_op jit(solution)/shard_map/ppermute | solution.py:309
